TPU v7x, 32 devices: a whole 2x2x4 slice. The times are simulated.
32 devices in a mesh: groups: 2 (over x), seq: 16 (over z, y, core).
Axes of the slice: x: 2, y: 2, z: 4, core: 2. Of those that a mesh axis runs over, the one named last changes fastest.
Arguments:
- features: bfloat16 [4, 8192, 768], P('groups', 'seq'), parts along dimension 0, may hold values from -6 to 6
- gain_first: float32 [768], replicated, may hold values from 0.1 to 1.9
- kernel_first: float32 [5, 768], replicated, may hold values from -2.5 to 2.5
- weight_first: bfloat16 [768, 768], replicated, may hold values from -0.21875 to 0.21875
- bias_first: float32 [768], replicated, may hold values from -3 to 3
- gain_second: float32 [768], replicated, may hold values from 0.1 to 1.9
- kernel_second: float32 [5, 768], replicated, may hold values from -2.5 to 2.5
- weight_second: bfloat16 [768, 896], replicated, may hold values from -0.21875 to 0.21875
- bias_second: float32 [896], replicated, may hold values from -3 to 3
- cotangent: bfloat16 [4, 2048, 896], P('groups', 'seq'), parts along dimension 0, may hold values from -6 to 6
Outputs:
- grad_features: bfloat16 [4, 8192, 768], P('groups', 'seq'), parts along dimension 0
- grad_weight_first: float32 [1536, 768], P('groups', 'seq'), parts along dimension 0
- grad_weight_second: float32 [1536, 896], P('groups', 'seq'), parts along dimension 0
- grad_bias_first: float32 [1536], P('groups'), parts along dimension 0
- grad_bias_second: float32 [1792], P('groups'), parts along dimension 0
- grad_kernel_first: float32 [10, 768], P('groups'), parts along dimension 0
- grad_kernel_second: float32 [10, 768], P('groups'), parts along dimension 0
- grad_gain_first: float32 [1536], P('groups'), parts along dimension 0
- grad_gain_second: float32 [1536], P('groups'), parts along dimension 0
There are 2 independent parts, one for each index of `groups`. A program takes and returns all parts, laid end to end along the dimension named above; an argument that names none is the same for every part. Nothing has to cross between parts.
All inputs are finite; a program needn't handle non-finite values.
Results may differ from a plain program's by a relative error of at most 0.0067.
Values may be sent and summed in bfloat16 or wider, within the bound.
A program may use at most 128 MiB of HBM per device.

v0:
```python
import math

import jax
import jax.numpy as jnp
from jax import lax
from jax.sharding import PartitionSpec as P

epsilon = 1e-06
inv_sqrt_two = 0.7071067811865476
inv_sqrt_tau = 0.3989422804014327


def with_halo(shard, sides, width):
    for axis, dim in sides:
        devices, length = (lax.axis_size(axis), shard.shape[dim])
        up = [(i, (i + 1) % devices) for i in range(devices - 1)]
        down = [(j, i) for i, j in up]
        last = lax.slice_in_dim(shard, length - width, length, axis=dim)
        leading = lax.slice_in_dim(shard, 0, width, axis=dim)
        before = lax.ppermute(last, axis, up)
        after = lax.ppermute(leading, axis, down)
        shard = jnp.concatenate([before, shard, after], axis=dim)
    return shard


def gelu_pair(inputs):
    normal_cdf = 0.5 * (1.0 + jax.scipy.special.erf(inputs * inv_sqrt_two))
    density = jnp.exp(-0.5 * inputs * inputs) * inv_sqrt_tau
    return (inputs * normal_cdf, normal_cdf + inputs * density)


def rms_forward(values, gain_vec):
    factor = lax.rsqrt(jnp.mean(values * values, axis=-1, keepdims=True) + epsilon)
    return (values * factor * gain_vec, factor)


def rms_backward(values, factor, gain_vec, grad_norm):
    scaled = grad_norm * gain_vec
    inner = jnp.mean(scaled * values, axis=-1, keepdims=True)
    return factor * scaled - values * (factor * factor * factor) * inner


def taps_forward(padded, kernel, extent):
    total = kernel[0] * padded[:, 0:extent]
    for offset in range(1, 5):
        total = total + kernel[offset] * padded[:, offset : offset + extent]
    return total


def taps_backward(padded, kernel, extent):
    total = kernel[0] * padded[:, 4 : 4 + extent]
    for offset in range(1, 5):
        total = total + kernel[offset] * padded[:, 4 - offset : 4 - offset + extent]
    return total


def taps_kernel(padded, grad_conv, extent):
    return jnp.stack(
        [
            jnp.sum(padded[:, offset : offset + extent] * grad_conv, axis=(0, 1))
            for offset in range(5)
        ]
    )


def project(matrix, weight):
    flat = matrix.reshape(-1, matrix.shape[-1])
    return jnp.dot(flat, weight, preferred_element_type=jnp.float32).reshape(
        matrix.shape[0], matrix.shape[1], weight.shape[1]
    )


def project_back(matrix, weight):
    flat = matrix.reshape(-1, matrix.shape[-1])
    return jnp.dot(flat, weight.T, preferred_element_type=jnp.float32).reshape(
        matrix.shape[0], matrix.shape[1], weight.shape[0]
    )


def weight_grad(matrix, other):
    flat_left = matrix.reshape(-1, matrix.shape[-1])
    flat_right = other.reshape(-1, other.shape[-1])
    return lax.dot_general(
        flat_left, flat_right, (((0,), (0,)), ((), ())), preferred_element_type=jnp.float32
    )


def pool_pairs(values):
    return (values[:, 0::2] + values[:, 1::2]) * 0.5


def spread_pairs(values):
    return jnp.repeat(values * 0.5, 2, axis=1)


def per_device(
    features,
    gain_first,
    kernel_first,
    weight_first,
    bias_first,
    gain_second,
    kernel_second,
    weight_second,
    bias_second,
    cotangent,
):
    channels = features.shape[2]
    positions = features.shape[1]
    pooled_len = positions // 2
    norm_scale = 1.0 / math.sqrt(features.shape[0] * positions * lax.axis_size("seq"))
    widened = with_halo(features, (("seq", 1),), 2)
    margin = 0
    rim_width = margin + 2
    wide_values = widened.astype(jnp.float32)
    norm_wide, factor_wide = rms_forward(wide_values, gain_first)
    conv_wide = taps_forward(norm_wide, kernel_first, positions + 2 * margin).astype(jnp.bfloat16)
    pre_wide = project(conv_wide, weight_first) + bias_first
    act_wide, slope_wide = gelu_pair(pre_wide)
    pooled_wide = pool_pairs(wide_values[:, 2 : 2 + positions + 2 * margin] + act_wide).astype(
        jnp.bfloat16
    )
    pooled_rim = with_halo(pooled_wide, (("seq", 1),), 2)
    values = wide_values[:, rim_width : rim_width + positions]
    factor_first = factor_wide[:, rim_width : rim_width + positions]
    pooled_rim_f = pooled_rim.astype(jnp.float32)
    norm_second_rim, factor_rim = rms_forward(pooled_rim_f, gain_second)
    conv_second = taps_forward(norm_second_rim, kernel_second, pooled_len).astype(jnp.bfloat16)
    pre_second = project(conv_second, weight_second) + bias_second
    unused, slope_second = gelu_pair(pre_second)
    pooled_f = pooled_rim_f[:, 2 : 2 + pooled_len]
    factor_second = factor_rim[:, 2 : 2 + pooled_len]
    up_second = spread_pairs(cotangent.astype(jnp.float32))
    back_second = (up_second * slope_second).astype(jnp.bfloat16)
    term_second = weight_grad(conv_second, back_second) * norm_scale
    bias_term_second = jnp.sum(back_second.astype(jnp.float32), axis=(0, 1)) * norm_scale
    into_second = project_back(back_second, weight_second).astype(jnp.bfloat16)
    into_second_rim = with_halo(into_second, (("seq", 1),), 2).astype(jnp.float32)
    dnorm_second = taps_backward(into_second_rim, kernel_second, pooled_len)
    kernel_term_second = (
        taps_kernel(norm_second_rim, into_second.astype(jnp.float32), pooled_len) * norm_scale
    )
    gain_term_second = jnp.sum(dnorm_second * pooled_f * factor_second, axis=(0, 1)) * norm_scale
    dpooled = (
        rms_backward(pooled_f, factor_second, gain_second, dnorm_second)
        + up_second[:, :, :channels]
    )
    up_first = spread_pairs(dpooled)
    back_first = (up_first * slope_wide).astype(jnp.bfloat16)
    term_first = weight_grad(conv_wide, back_first) * norm_scale
    bias_term_first = jnp.sum(back_first.astype(jnp.float32), axis=(0, 1)) * norm_scale
    into_first = project_back(back_first, weight_first).astype(jnp.bfloat16)
    into_first_rim = with_halo(into_first, (("seq", 1),), 2).astype(jnp.float32)
    dnorm_first = taps_backward(into_first_rim, kernel_first, positions)
    kernel_term_first = (
        taps_kernel(norm_wide, into_first.astype(jnp.float32), positions) * norm_scale
    )
    gain_term_first = jnp.sum(dnorm_first * values * factor_first, axis=(0, 1)) * norm_scale
    grad_features = (up_first + rms_backward(values, factor_first, gain_first, dnorm_first)).astype(
        jnp.bfloat16
    )
    grad_weight_first, grad_weight_second = (
        lax.psum_scatter(term_first, "seq", scatter_dimension=1, tiled=True),
        lax.psum_scatter(term_second, "seq", scatter_dimension=1, tiled=True),
    )
    (
        grad_bias_first,
        grad_bias_second,
        grad_kernel_first,
        grad_kernel_second,
        grad_gain_first,
        grad_gain_second,
    ) = lax.psum(
        (
            bias_term_first,
            bias_term_second,
            kernel_term_first,
            kernel_term_second,
            gain_term_first,
            gain_term_second,
        ),
        "seq",
    )
    return (
        grad_features,
        grad_weight_first,
        grad_weight_second,
        grad_bias_first,
        grad_bias_second,
        grad_kernel_first,
        grad_kernel_second,
        grad_gain_first,
        grad_gain_second,
    )


def solution(mesh):
    return jax.shard_map(
        per_device,
        mesh=mesh,
        in_specs=(
            P("groups", "seq", None),
            P(),
            P(),
            P(),
            P(),
            P(),
            P(),
            P(),
            P(),
            P("groups", "seq", None),
        ),
        out_specs=(
            P("groups", "seq", None),
            P("groups", "seq"),
            P("groups", "seq"),
            P("groups"),
            P("groups"),
            P("groups", None),
            P("groups", None),
            P("groups"),
            P("groups"),
        ),
        check_vma=False,
    )
```

profile of v0, /device:TPU:0, one launch (start us, length us, event | category | flops | bytes accessed | tf_op | source)
XLA Modules:
  0.0 232.4 jit_solution(13257593811837979982)
XLA Ops:
  7.3 0.9 fusion.44
  8.2 2.4 %collective-permute-start = (bf16[2,2,768]{2,1,0:T(2,128)(2,1)S(1)}, bf16[2,2,768]{2,1,0:T(2,128)(2,1)S(1)}, u32[]{:S(2)}, u32[]{:S(2)}) collective-permute-start(bf16[2,2,768]{2,1,0:T(2,128)(2,1)S(1)} %get-tuple-element.45), channel_id=1, source_target_pairs={{0,1},{1,2},{2,3},{3,4},{4,5},{5,6},{6,7},{7,8},{8,9},{9,10},{10,1... | collective-permute-start | bytes 18440 | tf_op jit(solution)/shard_map/ppermute | solution.py:20
  10.5 1.3 collective-permute-start.1
  11.8 2.0 convert_multiply_fusion.10
  13.9 1.0 slice_reduce_fusion.9
  14.8 0.9 collective-permute-done.1
  15.7 2.0 multiply_reduce_fusion
  17.8 0.6 multiply_multiply_fusion.1
  18.4 1.9 add_convert_fusion.1
  20.3 0.3 maximum_convert_fusion
  20.6 0.8 copy-done.6
  21.4 0.7 copy-done.10
  22.1 4.1 %multiply_add_fusion = (f32[2,512,768]{2,1,0:T(8,128)}, f32[2,512,768]{2,1,0:T(8,128)}) fusion(f32[2,516,768]{2,1,0:T(8,128)S(1)} %maximum_convert_fusion, f32[768]{0:T(1024)S(1)} %copy-done.14, bf16[2,512,768]{2,1,0:T(8,128)(2,1)S(1)} %add_convert_fusion.1, bf16[768,768]{1,0:T(8,128)(2,1)S(1)} %copy-done.10), kind=kOutput, calls=%fused_computation.37 | convolution fusion | flops 1212678144 | bytes 12192768 | tf_op jit(solution)/shard_map/dot_general | solution.py:68
  26.2 8.6 %slice.169 = f32[2,256,768]{2,1,0:T(8,128)} slice(f32[2,512,768]{2,1,0:T(8,128)} %get-tuple-element.59), slice={[0:2:1], [0:512:2], [0:768:1]} | slice | bytes 3145728 | tf_op jit(solution)/shard_map/slice | solution.py:89
  34.8 8.6 %slice.170 = f32[2,256,768]{2,1,0:T(8,128)} slice(f32[2,512,768]{2,1,0:T(8,128)} %get-tuple-element.59), slice={[0:2:1], [1:512:2], [0:768:1]} | slice | bytes 3145728 | tf_op jit(solution)/shard_map/slice | solution.py:89
  43.4 2.2 multiply_convert_fusion
  45.6 4.3 %collective-permute-start.2 = (bf16[2,2,768]{2,1,0:T(2,128)(2,1)S(1)}, bf16[2,2,768]{2,1,0:T(2,128)(2,1)S(1)}, u32[]{:S(2)}, u32[]{:S(2)}) collective-permute-start(bf16[2,2,768]{2,1,0:T(2,128)(2,1)S(1)} %get-tuple-element.49), channel_id=1, source_target_pairs={{0,1},{1,2},{2,3},{3,4},{4,5},{5,6},{6,7},{7,8},{8,9},{9,10},{10,1... | collective-permute-start | bytes 18440 | tf_op jit(solution)/shard_map/ppermute | solution.py:20
  49.9 1.3 collective-permute-start.3
  51.2 1.9 broadcast_in_dim.4
  53.1 3.5 %reshape.108 = f32[2,256,896]{2,1,0:T(8,128)} reshape(f32[2,128,2,896]{3,2,1,0:T(2,128)} %broadcast_in_dim.4) | data formatting | bytes 3670016 | tf_op jit(solution)/shard_map/reshape | solution.py:93
  56.6 0.4 multiply_reduce_fusion.3
  56.9 0.3 multiply_multiply_fusion.3
  57.3 0.9 add_convert_fusion.2
  58.2 0.6 copy-done.5
  58.8 1.6 convert_reduce_fusion.1
  60.4 1.7 fusion.25
  62.1 4.3 %collective-permute-start.4 = (bf16[2,2,768]{2,1,0:T(2,128)(2,1)S(1)}, bf16[2,2,768]{2,1,0:T(2,128)(2,1)S(1)}, u32[]{:S(2)}, u32[]{:S(2)}) collective-permute-start(bf16[2,2,768]{2,1,0:T(2,128)(2,1)S(1)} %get-tuple-element.47), channel_id=1, source_target_pairs={{0,1},{1,2},{2,3},{3,4},{4,5},{5,6},{6,7},{7,8},{8,9},{9,10},{10,1... | collective-permute-start | bytes 18440 | tf_op jit(solution)/shard_map/ppermute | solution.py:20
  66.3 1.5 collective-permute-start.5
  67.9 0.2 maximum_convert_fusion.2
  68.1 2.6 %collective-permute-done.5 = bf16[2,2,768]{2,1,0:T(2,128)(2,1)S(1)} collective-permute-done((bf16[2,2,768]{2,1,0:T(2,128)(2,1)S(1)}, bf16[2,2,768]{2,1,0:T(2,128)(2,1)S(1)}, u32[]{:S(2)}, u32[]{:S(2)}) %collective-permute-start.5) | collective-permute-done | bytes 6176 | tf_op jit(solution)/shard_map/ppermute | solution.py:21
  70.6 0.2 maximum_convert_fusion.3
  70.8 1.7 multiply_reduce_fusion.4
  72.5 0.5 fusion.26
  73.1 2.7 %broadcast_in_dim.5 = f32[2,256,2,768]{3,2,1,0:T(2,128)} broadcast(f32[2,256,768]{2,1,0:T(8,128)S(1)} %fusion.26), dimensions={0,1,3} | broadcast | bytes 4718592 | tf_op jit(solution)/shard_map/broadcast_in_dim | solution.py:93
  75.8 5.3 %reshape.109 = f32[2,512,768]{2,1,0:T(8,128)} reshape(f32[2,256,2,768]{3,2,1,0:T(2,128)} %broadcast_in_dim.5) | data formatting | bytes 6291456 | tf_op jit(solution)/shard_map/reshape | solution.py:93
  81.1 3.7 %convert_reduce_fusion = (f32[768]{0:T(1024)S(1)}, bf16[2,512,768]{2,1,0:T(8,128)(2,1)S(1)}) fusion(f32[2,512,768]{2,1,0:T(8,128)} %reshape.109, f32[2,512,768]{2,1,0:T(8,128)} %get-tuple-element.60, f32[768]{0:T(1024)S(1)} %copy-done.14), kind=kLoop, calls=%fused_computation.34 | loop fusion | flops 10222848 | bytes 7870464 | tf_op jit(solution)/shard_map/reduce_sum | solution.py:151
  84.8 1.1 copy-done.9
  85.9 2.9 %bitcast_multiply_fusion.1 = f32[768,768]{0,1:T(8,128)} fusion(bf16[2,512,768]{2,1,0:T(8,128)(2,1)S(1)} %copy-done.7, bf16[2,512,768]{2,1,0:T(8,128)(2,1)S(1)} %get-tuple-element.40), kind=kOutput, calls=%fused_computation.42 | convolution fusion | flops 1208549376 | bytes 5505024 | tf_op jit(solution)/shard_map/dot_general | solution.py:83
  88.9 3.7 %bitcast_multiply_fusion = f32[768,896]{0,1:T(8,128)} fusion(bf16[2,256,768]{2,1,0:T(8,128)(2,1)S(1)} %add_convert_fusion.2, bf16[2,256,896]{2,1,0:T(8,128)(2,1)} %copy-done.11), kind=kOutput, calls=%fused_computation.40 | convolution fusion | flops 705331200 | bytes 4456448 | tf_op jit(solution)/shard_map/dot_general | solution.py:83
  92.8 9.8 %fusion.10 = (f32[768]{0:T(1024)S(1)}, f32[768]{0:T(1024)S(1)}, f32[768]{0:T(1024)S(1)}, f32[768]{0:T(1024)S(1)}, f32[768]{0:T(1024)S(1)}, /*index=5*/bf16[2,512,768]{2,1,0:T(8,128)(2,1)S(1)}) fusion(f32[2,516,768]{2,1,0:T(8,128)} %copy-done.1, bf16[2,512,768]{2,1,0:T(8,128)(2,1)} %copy-done.9, bf16[768,768]{1,0:T(8,128)(2,1)} %param.13), kind=kOutput, calls=%fused_computation.18 | convolution fusion | flops 1217392896 | bytes 20069376 | tf_op jit(solution)/shard_map/dot_general | solution.py:75
  102.6 4.3 %collective-permute-start.6 = (bf16[2,2,768]{2,1,0:T(2,128)(2,1)S(1)}, bf16[2,2,768]{2,1,0:T(2,128)(2,1)S(1)}, u32[]{:S(2)}, u32[]{:S(2)}) collective-permute-start(bf16[2,2,768]{2,1,0:T(2,128)(2,1)S(1)} %get-tuple-element.43), channel_id=1, source_target_pairs={{0,1},{1,2},{2,3},{3,4},{4,5},{5,6},{6,7},{7,8},{8,9},{9,10},{10,1... | collective-permute-start | bytes 18440 | tf_op jit(solution)/shard_map/ppermute | solution.py:20
  106.9 1.5 collective-permute-start.7
  108.6 1.9 collective-permute-done.7
  110.5 0.3 maximum_convert_fusion.1
  110.9 4.3 %multiply_reduce_fusion.1 = (f32[768]{0:T(1024)S(1)}, f32[2,512]{1,0:T(2,128)S(1)}, f32[2,512,768]{2,1,0:T(8,128)}) fusion(f32[2,516,768]{2,1,0:T(8,128)S(1)} %copy-done.3, f32[2,512]{1,0:T(2,128)S(1)} %get-tuple-element.52, f32[768]{0:T(1024)S(1)} %copy-done.12, f32[2,516,768]{2,1,0:T(8,128)S(1)} %maximum_convert_fusion.1, f32[768]{0:T(1024)S(1)} %get-tuple-element.31, ...), kind=kLoop, calls=%fused_computation.28 | loop fusion | flops 11794688 | bytes 22049792 | tf_op jit(solution)/shard_map/reduce_sum | solution.py:158
  115.2 62.4 %all-reduce = (f32[768]{0:T(1024)}, f32[896]{0:T(1024)}, f32[5,768]{1,0:T(8,128)}, f32[5,768]{1,0:T(8,128)}, f32[768]{0:T(1024)}, /*index=5*/f32[768]{0:T(1024)}) all-reduce(f32[768]{0:T(1024)S(1)} %broadcast_multiply_fusion.5, f32[896]{0:T(1024)S(1)} %broadcast_multiply_fusion.2, ...), channel_id=1, replica_groups=mesh['groups'=2,'seq'=16] {'seq'}, use_global_device_ids=true, to_apply=%region_7.0 | all-reduce | flops 10880 | bytes 87040 | tf_op jit(solution)/shard_map/psum | solution.py:173
  177.6 5.4 %add_convert_fusion = bf16[2,512,768]{2,1,0:T(8,128)(2,1)} fusion(f32[2,512,768]{2,1,0:T(8,128)} %reshape.109, f32[2,512,768]{2,1,0:T(8,128)} %get-tuple-element.41, f32[2,516,768]{2,1,0:T(8,128)} %copy-done.2, f32[2,512]{1,0:T(2,128)S(1)} %broadcast_multiply_fusion.6, f32[2,512]{1,0:T(2,128)S(1)} %get-tuple-element.51, f32[768]{0:T(1024)S(1)} %copy-done.12, ...), kind=kLoop, calls=%fused_computation.35 | loop fusion | flops 5505024 | bytes 11025408 | tf_op jit(solution)/shard_map/convert_element_type | solution.py:159
  183.0 42.6 %reduce-scatter.5.cloned.1.call-done = f32[768,56]{0,1:T(8,128)} async-done(((f32[768,896]{0,1:T(8,128)}), f32[768,56]{0,1:T(8,128)}) %reduce-scatter.5.cloned.1.call-update) | async-done | bytes 172048 | tf_op jit(solution)/shard_map/reduce_scatter | solution.py:164
  (66 shorter events, 0.6 us)
Async XLA Ops:
  7.2 51.0 %copy-start = (bf16[768,896]{1,0:T(8,128)(2,1)S(1)}, bf16[768,896]{1,0:T(8,128)(2,1)}, u32[]{:S(2)}) copy-start(bf16[768,896]{1,0:T(8,128)(2,1)} %param.17) | copy-start | bytes 4128772
  7.2 10.6 %copy-start.4 = (bf16[2,512,768]{2,1,0:T(8,128)(2,1)S(1)}, bf16[2,512,768]{2,1,0:T(8,128)(2,1)}, u32[]{:S(2)}) copy-start(bf16[2,512,768]{2,1,0:T(8,128)(2,1)} %param.10) | copy-start | bytes 4718596
  7.2 10.6 %copy-start.12 = (f32[768]{0:T(1024)S(1)}, f32[768]{0:T(1024)}, u32[]{:S(2)}) copy-start(f32[768]{0:T(1024)} %param.11) | copy-start | bytes 9220
  7.2 175.8 %reduce-scatter.3.cloned.1.call-start = ((), (), s32[]{:S(2)}) async-start(), calls=%async_computation.2 | async-start | bytes 2506752 | tf_op jit(solution)/shard_map/reduce_scatter | solution.py:163
  8.2 6.6 %collective-permute-start = (bf16[2,2,768]{2,1,0:T(2,128)(2,1)S(1)}, bf16[2,2,768]{2,1,0:T(2,128)(2,1)S(1)}, u32[]{:S(2)}, u32[]{:S(2)}) collective-permute-start(bf16[2,2,768]{2,1,0:T(2,128)(2,1)S(1)} %get-tuple-element.45), channel_id=1, source_target_pairs={{0,1},{1,2},{2,3},{3,4},{4,5},{5,6},{6,7},{7,8},{8,9},{9,10},{10,1... | collective-permute-start | bytes 18440 | tf_op jit(solution)/shard_map/ppermute | solution.py:20
  10.5 5.2 %collective-permute-start.1 = (bf16[2,2,768]{2,1,0:T(2,128)(2,1)S(1)}, bf16[2,2,768]{2,1,0:T(2,128)(2,1)S(1)}, u32[]{:S(2)}, u32[]{:S(2)}) collective-permute-start(bf16[2,2,768]{2,1,0:T(2,128)(2,1)S(1)} %get-tuple-element.46), channel_id=1, source_target_pairs={{1,0},{2,1},{3,2},{4,3},{5,4},{6,5},{7,6},{8,7},{9,8},{10,9},{11,1... | collective-permute-start | bytes 18440 | tf_op jit(solution)/shard_map/ppermute | solution.py:21
  18.4 1.9 copy-start.1
  20.3 1.1 copy-start.6
  20.3 1.8 copy-start.10
  20.3 1.8 copy-start.14
  22.1 4.1 %copy-start.2 = (f32[2,516,768]{2,1,0:T(8,128)}, f32[2,516,768]{2,1,0:T(8,128)S(1)}, u32[]{:S(2)}) copy-start(f32[2,516,768]{2,1,0:T(8,128)S(1)} %maximum_convert_fusion) | copy-start | bytes 9510916
  43.4 7.8 %copy-start.15 = (f32[5,768]{1,0:T(8,128)S(1)}, f32[5,768]{1,0:T(8,128)}, u32[]{:S(2)}) copy-start(f32[5,768]{1,0:T(8,128)} %param.16) | copy-start | bytes 46084
  43.4 7.9 %copy-start.8 = (f32[2,128,896]{2,1,0:T(8,128)S(1)}, f32[2,128,896]{2,1,0:T(8,128)}, u32[]{:S(2)}) copy-start(f32[2,128,896]{2,1,0:T(8,128)} %convert_multiply_fusion.10) | copy-start | bytes 2752516
  45.6 11.0 %collective-permute-start.2 = (bf16[2,2,768]{2,1,0:T(2,128)(2,1)S(1)}, bf16[2,2,768]{2,1,0:T(2,128)(2,1)S(1)}, u32[]{:S(2)}, u32[]{:S(2)}) collective-permute-start(bf16[2,2,768]{2,1,0:T(2,128)(2,1)S(1)} %get-tuple-element.49), channel_id=1, source_target_pairs={{0,1},{1,2},{2,3},{3,4},{4,5},{5,6},{6,7},{7,8},{8,9},{9,10},{10,1... | collective-permute-start | bytes 18440 | tf_op jit(solution)/shard_map/ppermute | solution.py:20
  49.9 6.7 %collective-permute-start.3 = (bf16[2,2,768]{2,1,0:T(2,128)(2,1)S(1)}, bf16[2,2,768]{2,1,0:T(2,128)(2,1)S(1)}, u32[]{:S(2)}, u32[]{:S(2)}) collective-permute-start(bf16[2,2,768]{2,1,0:T(2,128)(2,1)S(1)} %get-tuple-element.50), channel_id=1, source_target_pairs={{1,0},{2,1},{3,2},{4,3},{5,4},{6,5},{7,6},{8,7},{9,8},{10,9},{11,1... | collective-permute-start | bytes 18440 | tf_op jit(solution)/shard_map/ppermute | solution.py:21
  53.1 3.8 %copy-start.13 = (f32[768]{0:T(1024)S(1)}, f32[768]{0:T(1024)}, u32[]{:S(2)}) copy-start(f32[768]{0:T(1024)} %param.15) | copy-start | bytes 9220
  57.3 1.5 copy-start.5
  57.3 1.5 copy-start.16
  60.3 1.7 copy-start.11
  62.1 6.0 %collective-permute-start.4 = (bf16[2,2,768]{2,1,0:T(2,128)(2,1)S(1)}, bf16[2,2,768]{2,1,0:T(2,128)(2,1)S(1)}, u32[]{:S(2)}, u32[]{:S(2)}) collective-permute-start(bf16[2,2,768]{2,1,0:T(2,128)(2,1)S(1)} %get-tuple-element.47), channel_id=1, source_target_pairs={{0,1},{1,2},{2,3},{3,4},{4,5},{5,6},{6,7},{7,8},{8,9},{9,10},{10,1... | collective-permute-start | bytes 18440 | tf_op jit(solution)/shard_map/ppermute | solution.py:20
  66.3 4.3 %collective-permute-start.5 = (bf16[2,2,768]{2,1,0:T(2,128)(2,1)S(1)}, bf16[2,2,768]{2,1,0:T(2,128)(2,1)S(1)}, u32[]{:S(2)}, u32[]{:S(2)}) collective-permute-start(bf16[2,2,768]{2,1,0:T(2,128)(2,1)S(1)} %get-tuple-element.48), channel_id=1, source_target_pairs={{1,0},{2,1},{3,2},{4,3},{5,4},{6,5},{7,6},{8,7},{9,8},{10,9},{11,1... | collective-permute-start | bytes 18440 | tf_op jit(solution)/shard_map/ppermute | solution.py:21
  81.1 4.9 %copy-start.7 = (bf16[2,512,768]{2,1,0:T(8,128)(2,1)S(1)}, bf16[2,512,768]{2,1,0:T(8,128)(2,1)}, u32[]{:S(2)}) copy-start(bf16[2,512,768]{2,1,0:T(8,128)(2,1)} %copy-done.6) | copy-start | bytes 4718596
  84.8 1.1 copy-start.9
  88.9 136.7 %reduce-scatter.5.cloned.1.call-start = ((), (), s32[]{:S(2)}) async-start(), calls=%async_computation.3 | async-start | bytes 2924544 | tf_op jit(solution)/shard_map/reduce_scatter | solution.py:164
  102.6 6.0 %collective-permute-start.6 = (bf16[2,2,768]{2,1,0:T(2,128)(2,1)S(1)}, bf16[2,2,768]{2,1,0:T(2,128)(2,1)S(1)}, u32[]{:S(2)}, u32[]{:S(2)}) collective-permute-start(bf16[2,2,768]{2,1,0:T(2,128)(2,1)S(1)} %get-tuple-element.43), channel_id=1, source_target_pairs={{0,1},{1,2},{2,3},{3,4},{4,5},{5,6},{6,7},{7,8},{8,9},{9,10},{10,1... | collective-permute-start | bytes 18440 | tf_op jit(solution)/shard_map/ppermute | solution.py:20
  106.9 3.6 %collective-permute-start.7 = (bf16[2,2,768]{2,1,0:T(2,128)(2,1)S(1)}, bf16[2,2,768]{2,1,0:T(2,128)(2,1)S(1)}, u32[]{:S(2)}, u32[]{:S(2)}) collective-permute-start(bf16[2,2,768]{2,1,0:T(2,128)(2,1)S(1)} %get-tuple-element.44), channel_id=1, source_target_pairs={{1,0},{2,1},{3,2},{4,3},{5,4},{6,5},{7,6},{8,7},{9,8},{10,9},{11,1... | collective-permute-start | bytes 18440 | tf_op jit(solution)/shard_map/ppermute | solution.py:21
  108.6 2.3 copy-start.3
Sparse Core Ops, SparseCore 0:
  89.0 68.1 reduce-scatter.2
  162.0 63.5 reduce-scatter.4
where the time goes:
time: 234 us; the launch traced here: 232 us
  blocking collectives  62.4 us (27%)
  waiting for transfers between devices  48.1 us (21%)
  local copies, waits for them, and re-layouts  35.8 us (15%)
  other arithmetic  27 us (12%)
  matrix products  23.7 us (10%)
  starting transfers between devices  20.8 us (9%)
  between operations  14.5 us (6%)
    psum x1, blocking collectives, per_device(): lax.psum((bias_term_first, bias_term_second, kernel_term_first, kernel_te...  62.4 us
    reduce_scatter x1, waiting for transfers between devices, per_device(): lax.psum_scatter(term_second, 'seq', scatter_dimension=1, tiled=True)  42.6 us
    slice x2, local copies, waits for them, and re-layouts, pool_pairs(): return (values[:, 0::2] + values[:, 1::2]) * 0.5  17.2 us
    ppermute x4, starting transfers between devices, with_halo(): before = lax.ppermute(last, axis, up)  15.2 us
    dot_general x2, matrix products, project_back(): jnp.dot(flat, weight.T, preferred_element_type=jnp.float32)  11.4 us
    reshape x2, local copies, waits for them, and re-layouts, spread_pairs(): return jnp.repeat(values * 0.5, 2, axis=1)  8.74 us
    dot_general x2, matrix products, weight_grad(): lax.dot_general(flat_left, flat_right, (((0,), (0,)), ((), ())), preferre...  6.6 us
    dot_general x2, matrix products, project(): jnp.dot(flat, weight, preferred_element_type=jnp.float32)  5.65 us
  transfers between devices with their start and end apart: 10, of which 4 were waited for; matrix products, arithmetic and copies ran while one was open for 14% of the time, Pallas kernels for 0%

commit v1 on v0

v1 whole, which is shorter than its diff:
```python
import functools
import math

import jax
import jax.numpy as jnp
from jax import lax
from jax.experimental import pallas as pl
from jax.experimental.pallas import tpu as pltpu
from jax.sharding import PartitionSpec as P

MESH = pl.DeviceIdType.MESH
F32 = jnp.float32
BF16 = jnp.bfloat16
epsilon = 1e-06
inv_sqrt_two = 0.7071067811865476
inv_sqrt_tau = 0.3989422804014327
HALO = 16
LANES = 128


def gelu_parts(v):
    cdf = 0.5 * (1.0 + lax.erf(v * inv_sqrt_two))
    return cdf, jnp.exp(-0.5 * v * v) * inv_sqrt_tau


def extend(planes):
    m, rows = len(planes), planes[0].shape[0]
    down = [pltpu.roll(planes[i], 1, 0) for i in (m - 2, m - 1)]
    up = [pltpu.roll(planes[i], rows - 1, 0) for i in (0, 1)]
    return down + planes + up


def halo_kernel(n, x_ref, c_ref, xb_ref, xa_ref, cb_ref, ca_ref, send_sem, recv_sem):
    me = lax.axis_index("seq")
    right, left = lax.rem(me + 1, n), lax.rem(me + n - 1, n)
    barrier = pltpu.get_barrier_semaphore()
    for other in (left, right):
        pl.semaphore_signal(barrier, inc=1, device_id={"seq": other}, device_id_type=MESH)
    pl.semaphore_wait(barrier, 2)
    copies = []
    for ref, before, after in ((x_ref, xb_ref, xa_ref), (c_ref, cb_ref, ca_ref)):
        length = ref.shape[1]
        for source, target, other in (
            (ref.at[:, pl.ds(length - HALO, HALO)], before, right),
            (ref.at[:, pl.ds(0, HALO)], after, left),
        ):
            k = len(copies)
            copies.append(
                pltpu.make_async_remote_copy(
                    src_ref=source,
                    dst_ref=target,
                    send_sem=send_sem.at[k],
                    recv_sem=recv_sem.at[k],
                    device_id={"seq": other},
                    device_id_type=MESH,
                )
            )
            copies[-1].start()
    for copy in copies:
        copy.wait()


def local_kernel(
    scale,
    blocks,
    edge_ref,
    x_ref,
    xb_ref,
    xa_ref,
    c_ref,
    cb_ref,
    ca_ref,
    g1_ref,
    k1_ref,
    w1_ref,
    b1_ref,
    g2_ref,
    k2_ref,
    w2_ref,
    b2_ref,
    out_ref,
    *rest,
):
    if blocks:
        blk_ref, small_ref = rest[:2]
        rest = rest[2:]
    else:
        gt1_ref, gt2_ref, small_ref = rest[:3]
        rest = rest[3:]
    (xs, xp, fac, conv, slope, up, fac2, conv2, back2, own2, into2, cot, ss, own, inside,
     back, own1, into, dn, gt) = rest
    batch, length, ch = x_ref.shape
    ch2 = c_ref.shape[2]
    span = length + 2 * HALO
    per = span // 4
    rows = batch * per
    groups = ch // LANES
    side = HALO // 4

    within = lax.broadcasted_iota(jnp.int32, (rows, LANES), 0)
    for b in range(1, batch):
        within = jnp.where(within >= per, within - per, within)
    is_own = (within >= side) & (within < per - side)
    own[...] = jnp.where(is_own, 1.0, 0.0)
    low = jnp.where(edge_ref[0] == 1, side, 0)
    high = jnp.where(edge_ref[1] == 1, per - side, per)
    inside[...] = jnp.where((within >= low) & (within < high), 1.0, 0.0)
    at_first, at_last = edge_ref[0] == 1, edge_ref[1] == 1

    for b in range(batch):
        base = b * per
        first = cb_ref[b].astype(F32)[HALO - side :] * 0.5
        last = ca_ref[b].astype(F32)[:side] * 0.5
        cot[base : base + side] = jnp.where(at_first, 0.0, first)
        cot[base + side : base + per - side] = c_ref[b].astype(F32) * 0.5
        cot[base + per - side : base + per] = jnp.where(at_last, 0.0, last)

    def lanes(c, width=LANES):
        return pl.ds(pl.multiple_of(c * width, width), width)

    ss[...] = jnp.zeros_like(ss)

    @pl.loop(0, groups)
    def _(c):
        for b in range(batch):
            base = b * span
            xs[c, base : base + HALO] = jnp.where(at_first, 0.0, xb_ref[b, :, lanes(c)].astype(F32))
            xs[c, base + HALO : base + HALO + length] = x_ref[b, :, lanes(c)].astype(F32)
            xs[c, base + HALO + length : base + span] = jnp.where(
                at_last, 0.0, xa_ref[b, :, lanes(c)].astype(F32)
            )
        for r in range(4):
            v = xs[c, pl.ds(r, rows, stride=4), :]
            xp[r * rows : (r + 1) * rows, lanes(c)] = v
            ss[r * rows : (r + 1) * rows] += v * v

    fac[...] = jnp.broadcast_to(
        lax.rsqrt(jnp.sum(ss[...], axis=1, keepdims=True) * (1.0 / ch) + epsilon), fac.shape
    )

    def normed(values, factors, gain_ref, c, m):
        gain = gain_ref[:, lanes(c)]
        return [
            values[r * rows : (r + 1) * rows, lanes(c)] * factors[r * rows : (r + 1) * rows] * gain
            for r in range(m)
        ]

    def taps(c, m, values, factors, gain_ref, kernel_ref, target):
        ext = extend(normed(values, factors, gain_ref, c, m))
        k = [kernel_ref[j : j + 1, lanes(c)] for j in range(5)]
        for r in range(m):
            total = k[0] * ext[r]
            for j in range(1, 5):
                total = total + k[j] * ext[r + j]
            target[r * rows : (r + 1) * rows, lanes(c)] = total.astype(BF16)

    pl.loop(0, groups)(lambda c: taps(c, 4, xp, fac, g1_ref, k1_ref, conv))

    wide = 256

    for t in range(2):

        @pl.loop(0, ch // wide)
        def _(n):
            part = lanes(n, wide)
            pre = jnp.dot(
                conv[2 * t * rows : 2 * (t + 1) * rows], w1_ref[:, part], preferred_element_type=F32
            )
            pre = pre + b1_ref[:, part]
            cdf, density = gelu_parts(pre)
            slope[2 * t * rows : 2 * (t + 1) * rows, part] = cdf + pre * density
            s = xp[2 * t * rows : 2 * (t + 1) * rows, part] + pre * cdf
            pooled = (s[:rows] + s[rows:]) * 0.5
            mask = inside[...]
            mask = jnp.concatenate([mask] * (wide // LANES), axis=1)
            up[t * rows : (t + 1) * rows, part] = (pooled.astype(BF16).astype(F32)) * mask

    total = jnp.zeros((2 * rows, LANES), F32)
    for c in range(groups):
        v = up[:, c * LANES : (c + 1) * LANES]
        total = total + v * v
    fac2[...] = jnp.broadcast_to(
        lax.rsqrt(jnp.sum(total, axis=1, keepdims=True) * (1.0 / ch) + epsilon), fac2.shape
    )
    pl.loop(0, groups)(lambda c: taps(c, 2, up, fac2, g2_ref, k2_ref, conv2))

    @pl.loop(0, ch2 // LANES)
    def _(n):
        part = lanes(n)
        pre = jnp.dot(conv2[...], w2_ref[:, part], preferred_element_type=F32) + b2_ref[:, part]
        cdf, density = gelu_parts(pre)
        grad = cot[:, part]
        total = jnp.zeros((1, LANES), F32)
        for t in range(2):
            at = slice(t * rows, (t + 1) * rows)
            value = (grad * (cdf[at] + pre[at] * density[at])).astype(BF16)
            back2[at, part] = value
            kept = value.astype(F32) * own[...]
            own2[at, part] = kept.astype(BF16)
            total = total + jnp.sum(kept, axis=0, keepdims=True)
        small_ref[14:15, part] = total * scale

    nt = (((1,), (1,)), ((), ()))
    tn = (((0,), (0,)), ((), ()))

    @pl.loop(0, ch // wide)
    def _(n):
        into2[:, lanes(n, wide)] = lax.dot_general(
            back2[...], w2_ref[lanes(n, wide), :], nt, preferred_element_type=F32
        ).astype(BF16)

    def weight_term(left, right, target_rows, offset, plain_ref):
        for s in range(0, left.shape[1], wide):
            e = min(s + wide, left.shape[1])
            gt[s:e] = (
                lax.dot_general(left[:, s:e], right[...], tn, preferred_element_type=F32) * scale
            )
        count = left.shape[1]
        if blocks:
            size = count // 16
            for d in range(16):
                z, y, core = d // 4, (d // 2) % 2, d % 2
                blk_ref[core, y, z, offset : offset + size, :] = gt[
                    d * size : (d + 1) * size
                ].astype(BF16)
        else:
            plain_ref[...] = gt[0:count]

    weight_term(own2, conv2, ch2, ch // 16, None if blocks else gt2_ref)

    def taps_back(c, m, values, factors, gain_ref, kernel_ref, grads, kernel_row, gain_row):
        norm = extend(normed(values, factors, gain_ref, c, m))
        g = [grads[r * rows : (r + 1) * rows, lanes(c)].astype(F32) for r in range(m)]
        ext = extend(g)
        k = [kernel_ref[j : j + 1, lanes(c)] for j in range(5)]
        gain = gain_ref[:, lanes(c)]
        mask = own[...]
        kept = [v * mask for v in g]
        gain_total = jnp.zeros((1, LANES), F32)
        for j in range(5):
            total = norm[j] * kept[0]
            for r in range(1, m):
                total = total + norm[r + j] * kept[r]
            small_ref[kernel_row + j : kernel_row + j + 1, lanes(c)] = (
                jnp.sum(total, axis=0, keepdims=True) * scale
            )
        gain_sum = None
        for r in range(m):
            at = slice(r * rows, (r + 1) * rows)
            d = k[0] * ext[r + 4]
            for j in range(1, 5):
                d = d + k[j] * ext[r + 4 - j]
            v = values[at, lanes(c)]
            dv = d * v
            term = dv * factors[at] * mask
            gain_sum = term if gain_sum is None else gain_sum + term
            ss[at] += dv * gain
            dn[at, lanes(c)] = d * gain
        small_ref[gain_row : gain_row + 1, lanes(c)] = (
            jnp.sum(gain_sum, axis=0, keepdims=True) * scale
        )

    ss[...] = jnp.zeros_like(ss)
    pl.loop(0, groups)(
        lambda c: taps_back(c, 2, up, fac2, g2_ref, k2_ref, into2, 5, 11)
    )
    f2 = fac2[...]
    inner2 = jnp.sum(ss[0 : 2 * rows], axis=1, keepdims=True) * (1.0 / ch)
    ss[0 : 2 * rows] = f2 * f2 * f2 * jnp.broadcast_to(inner2, f2.shape)

    @pl.loop(0, groups)
    def _(c):
        part = lanes(c)
        grad = cot[:, part]
        mask = inside[...] * 0.5
        total = jnp.zeros((1, LANES), F32)
        for t in range(2):
            at = slice(t * rows, (t + 1) * rows)
            d = fac2[at] * dn[at, part] - up[at, part] * ss[at] + grad
            d = d * mask
            up[at, part] = d
            for r in (2 * t, 2 * t + 1):
                to = slice(r * rows, (r + 1) * rows)
                value = (d * slope[to, part]).astype(BF16)
                back[to, part] = value
                kept = value.astype(F32) * own[...]
                own1[to, part] = kept.astype(BF16)
                total = total + jnp.sum(kept, axis=0, keepdims=True)
        small_ref[13:14, part] = total * scale

    @pl.loop(0, ch // wide)
    def _(n):
        into[:, lanes(n, wide)] = lax.dot_general(
            back[...], w1_ref[lanes(n, wide), :], nt, preferred_element_type=F32
        ).astype(BF16)

    weight_term(own1, conv, ch, 0, None if blocks else gt1_ref)

    ss[...] = jnp.zeros_like(ss)
    pl.loop(0, groups)(lambda c: taps_back(c, 4, xp, fac, g1_ref, k1_ref, into, 0, 10))
    f1 = fac[...]
    inner = jnp.sum(ss[...], axis=1, keepdims=True) * (1.0 / ch)
    ss[...] = f1 * f1 * f1 * jnp.broadcast_to(inner, f1.shape)
    small_ref[12:13, :] = jnp.zeros((1, small_ref.shape[1]), F32)
    small_ref[15:16, :] = jnp.zeros((1, small_ref.shape[1]), F32)
    small_ref[0:14, ch:] = jnp.zeros((14, small_ref.shape[1] - ch), F32)

    @pl.loop(0, groups)
    def _(c):
        part = lanes(c)
        for r in range(4):
            at = slice(r * rows, (r + 1) * rows)
            half = slice((r // 2) * rows, (r // 2 + 1) * rows)
            v = up[half, part] + fac[at] * dn[at, part] - xp[at, part] * ss[at]
            xs[c, pl.ds(r, rows, stride=4), :] = v
        for b in range(batch):
            base = b * span + HALO
            out_ref[b, :, part] = xs[c, base : base + length].astype(BF16)


def sum_kernel(blk, small, out_ref, small_out, recv1, kept, send2, recv2, send3, recv3, total,
               srecv1, ssend2, srecv2, sall, send_sem, recv_sem):
    g = lax.axis_index("seq")
    z, y, c = g // 4, lax.rem(g // 2, 2), lax.rem(g, 2)
    core = g + 1 - 2 * c
    over = g + 2 - 4 * y

    def hop(step):
        zt = lax.rem(z + step, 4)
        return zt, zt * 4 + y * 2 + c

    barrier = pltpu.get_barrier_semaphore()
    others = [core, over] + [hop(s)[1] for s in (1, 2, 3)]
    for other in others:
        pl.semaphore_signal(barrier, inc=1, device_id={"seq": other}, device_id_type=MESH)
    pl.semaphore_wait(barrier, 5)

    def send(k, source, target, other):
        copy = pltpu.make_async_remote_copy(
            src_ref=source,
            dst_ref=target,
            send_sem=send_sem.at[k],
            recv_sem=recv_sem.at[k],
            device_id={"seq": other},
            device_id_type=MESH,
        )
        copy.start()
        return copy

    small1 = send(0, small, srecv1, core)
    far = send(1, blk.at[1 - c, 1 - y], recv1.at[0], core)
    near = send(2, blk.at[1 - c, y], recv1.at[1], core)

    far.wait()
    steps = (2, 1, 3, 0)
    over_copies = []
    for i, step in enumerate(steps):
        zt, _ = hop(step)
        send2[i] = (blk[c, 1 - y, zt].astype(F32) + recv1[0, zt].astype(F32)).astype(BF16)
        over_copies.append(send(3 + i, send2.at[i], recv2.at[i], over))
        if i == 0:
            small1.wait()
            ssend2[...] = small[...] + srecv1[...]
            small2 = send(7, ssend2, srecv2, over)
    near.wait()
    for i, step in enumerate(steps):
        zt, _ = hop(step)
        kept[i] = blk[c, y, zt].astype(F32) + recv1[1, zt].astype(F32)

    z_copies = []
    for i, step in enumerate(steps):
        over_copies[i].wait()
        if i == 0:
            small2.wait()
            sall[z] = ssend2[...] + srecv2[...]
        if step:
            _, other = hop(step)
            send3[i] = (kept[i] + recv2[i].astype(F32)).astype(BF16)
            z_copies.append(send(8 + i, send3.at[i], recv3.at[i], other))
            z_copies.append(send(11 + i, sall.at[z], sall.at[z], other))
        else:
            total[...] = kept[i] + recv2[i].astype(F32)
    for copy in z_copies:
        copy.wait()
    result = total[...]
    for i in range(3):
        result = result + recv3[i].astype(F32)
    out_ref[...] = result
    small_out[...] = (sall[0] + sall[1]) + (sall[2] + sall[3])


def per_device(fast, n, x, g1, k1, w1, b1, g2, k2, w2, b2, cot):
    batch, length, ch = x.shape
    quarter, ch2 = cot.shape[1:]
    scale = 1.0 / math.sqrt(batch * length * n)
    any_spec = pl.BlockSpec(memory_space=pl.ANY)
    vmem = pl.BlockSpec(memory_space=pltpu.VMEM)

    xb, xa, cb, ca = pl.pallas_call(
        functools.partial(halo_kernel, n),
        out_shape=[jax.ShapeDtypeStruct((batch, HALO, ch), BF16)] * 2
        + [jax.ShapeDtypeStruct((batch, HALO, ch2), BF16)] * 2,
        in_specs=[any_spec] * 2,
        out_specs=[any_spec] * 4,
        scratch_shapes=[pltpu.SemaphoreType.DMA((4,)), pltpu.SemaphoreType.DMA((4,))],
        compiler_params=pltpu.CompilerParams(collective_id=0, has_side_effects=True),
        name="halo",
    )(x, cot)

    me = lax.axis_index("seq")
    edge = jnp.stack([me == 0, me == n - 1]).astype(jnp.int32)
    rows = batch * (length + 2 * HALO) // 4
    lead = (ch + ch2) // 16
    if fast:
        grads = [jax.ShapeDtypeStruct((2, 2, 4, lead, ch), BF16)]
    else:
        grads = [jax.ShapeDtypeStruct((ch, ch), F32), jax.ShapeDtypeStruct((ch2, ch), F32)]
    outs = pl.pallas_call(
        functools.partial(local_kernel, scale, fast),
        out_shape=[jax.ShapeDtypeStruct(x.shape, BF16)]
        + grads
        + [jax.ShapeDtypeStruct((16, ch2), F32)],
        in_specs=[pl.BlockSpec(memory_space=pltpu.SMEM)] + [vmem] * 14,
        out_specs=[vmem] * (2 + len(grads)),
        scratch_shapes=[
            pltpu.VMEM((ch // LANES, 4 * rows, LANES), F32),
            pltpu.VMEM((4 * rows, ch), F32),
            pltpu.VMEM((4 * rows, LANES), F32),
            pltpu.VMEM((4 * rows, ch), BF16),
            pltpu.VMEM((4 * rows, ch), F32),
            pltpu.VMEM((2 * rows, ch), F32),
            pltpu.VMEM((2 * rows, LANES), F32),
            pltpu.VMEM((2 * rows, ch), BF16),
            pltpu.VMEM((2 * rows, ch2), BF16),
            pltpu.VMEM((2 * rows, ch2), BF16),
            pltpu.VMEM((2 * rows, ch), BF16),
            pltpu.VMEM((rows, ch2), F32),
            pltpu.VMEM((4 * rows, LANES), F32),
            pltpu.VMEM((rows, LANES), F32),
            pltpu.VMEM((rows, LANES), F32),
            pltpu.VMEM((4 * rows, ch), BF16),
            pltpu.VMEM((4 * rows, ch), BF16),
            pltpu.VMEM((4 * rows, ch), BF16),
            pltpu.VMEM((4 * rows, ch), F32),
            pltpu.VMEM((max(ch, ch2), ch), F32),
        ],
        compiler_params=pltpu.CompilerParams(vmem_limit_bytes=56 * 2**20),
        name="local",
    )(
        edge, x, xb, xa, cot, cb, ca,
        g1[None], k1, w1, b1[None], g2[None], k2, w2, b2[None],
    )
    grad_x = outs[0]
    if fast:
        _, blk, small = outs
        total, small = pl.pallas_call(
            sum_kernel,
            out_shape=[
                jax.ShapeDtypeStruct((lead, ch), F32),
                jax.ShapeDtypeStruct(small.shape, F32),
            ],
            in_specs=[vmem] * 2,
            out_specs=[vmem] * 2,
            scratch_shapes=[
                pltpu.VMEM((2, 4, lead, ch), BF16),
                pltpu.VMEM((4, lead, ch), F32),
                pltpu.VMEM((4, lead, ch), BF16),
                pltpu.VMEM((4, lead, ch), BF16),
                pltpu.VMEM((3, lead, ch), BF16),
                pltpu.VMEM((3, lead, ch), BF16),
                pltpu.VMEM((lead, ch), F32),
                pltpu.VMEM(small.shape, F32),
                pltpu.VMEM(small.shape, F32),
                pltpu.VMEM(small.shape, F32),
                pltpu.VMEM((4,) + small.shape, F32),
                pltpu.SemaphoreType.DMA((14,)),
                pltpu.SemaphoreType.DMA((14,)),
            ],
            compiler_params=pltpu.CompilerParams(
                collective_id=1, has_side_effects=True, vmem_limit_bytes=40 * 2**20
            ),
            name="sums",
        )(blk, small)
        grad_w1, grad_w2 = total[: ch // 16].T, total[ch // 16 :].T
    else:
        _, gt1, gt2, small = outs
        grad_w1 = lax.psum_scatter(gt1, "seq", scatter_dimension=0, tiled=True).T
        grad_w2 = lax.psum_scatter(gt2, "seq", scatter_dimension=0, tiled=True).T
        small = lax.psum(small, "seq")
    return (
        grad_x,
        grad_w1,
        grad_w2,
        small[13, :ch],
        small[14],
        small[0:5, :ch],
        small[5:10, :ch],
        small[10, :ch],
        small[11, :ch],
    )


def solution(mesh):
    n = mesh.shape["seq"]
    return jax.shard_map(
        functools.partial(per_device, n == 16, n),
        mesh=mesh,
        in_specs=(P("groups", "seq", None),) + (P(),) * 8 + (P("groups", "seq", None),),
        out_specs=(
            P("groups", "seq", None),
            P("groups", "seq"),
            P("groups", "seq"),
            P("groups"),
            P("groups"),
            P("groups", None),
            P("groups", None),
            P("groups"),
            P("groups"),
        ),
        check_vma=False,
    )
```

time: 234 us -> 85.7 us (0.37)
  Pallas kernels: 0 us -> 73.3 us
  blocking collectives: 62.4 us -> 0 us
  waiting for transfers between devices: 48.1 us -> 0 us
  other arithmetic: 27 us -> 0.59 us
  local copies, waits for them, and re-layouts: 35.8 us -> 10.8 us
  matrix products: 23.7 us -> 0 us
  starting transfers between devices: 20.8 us -> 0 us
  between operations: 14.5 us -> 0.67 us
    pallas_call x0 -> x3, Pallas kernels: none -> 73.3 us  [the longest x1 32.6 us: per_device(): pl.pallas_call(functools.partial(local_kernel, scale, fast), out_shape=[j...]
    psum x1 -> x0, blocking collectives: 62.4 us -> none  [per_device(): lax.psum((bias_term_first, bias_term_second, kernel_term_first, kernel_te...]
    reduce_scatter x2 -> x0, waiting for transfers between devices: 42.6 us -> none  [the longest x1 42.6 us: per_device(): lax.psum_scatter(term_second, 'seq', scatter_dimension=1, tiled=True)]
    dot_general x6 -> x0, matrix products: 23.7 us -> none  [the longest x2 11.4 us: project_back(): jnp.dot(flat, weight.T, preferred_element_type=jnp.float32)]
    ppermute x8 -> x0, starting transfers between devices: 20.8 us -> none  [the longest x4 15.2 us: with_halo(): before = lax.ppermute(last, axis, up)]
    slice x8 -> x3, local copies, waits for them, and re-layouts: 19.1 us -> 1.85 us  [the longest x1 0.62 us: per_device(): small[11, :ch]]
    reduce_sum x5 -> x0, other arithmetic: 12.1 us -> none  [the longest x1 4.32 us: per_device(): jnp.sum(dnorm_first * values * factor_first, axis=(0, 1)) * norm_scale]
    convert_element_type x8 -> x1, other arithmetic: 11.3 us -> 0.59 us  [per_device(): edge = jnp.stack([me == 0, me == n - 1]).astype(jnp.int32)]
  transfers between devices with their start and end apart: 10 -> 0, of which waited for: 4 -> 0; matrix products, arithmetic and copies ran while one was open for 14% -> 0% of each run, Pallas kernels for 0% -> 0%
where the time goes in v1:
time: 85.7 us; the launch traced here: 85.3 us
  Pallas kernels  73.3 us (86%)
  local copies, waits for them, and re-layouts  10.8 us (13%)
    pallas_call x1, Pallas kernels, per_device(): pl.pallas_call(functools.partial(local_kernel, scale, fast), out_shape=[j...  32.6 us
    pallas_call x1, Pallas kernels, per_device(): pl.pallas_call(sum_kernel, out_shape=[jax.ShapeDtypeStruct((lead, ch), F3...  31.8 us
    pallas_call x1, Pallas kernels, per_device(): pl.pallas_call(functools.partial(halo_kernel, n), out_shape=[jax.ShapeDty...  8.89 us
    unnamed x4, local copies, waits for them, and re-layouts  2.54 us

profile of v1, /device:TPU:0, one launch (start us, length us, event | category | flops | bytes accessed | tf_op | source)
XLA Modules:
  0.0 85.3 jit_solution(5988590647379400381)
XLA Ops:
  0.6 0.6 add_convert_fusion.edge_ref
  1.2 1.3 %broadcast_in_dim.12.g1_ref = f32[1,768]{1,0:T(1,128)} reshape(f32[768]{0:T(1024)} %param.11) | data formatting | bytes 6144 | tf_op jit(solution)/shard_map/broadcast_in_dim | solution.py:451
  2.5 1.3 %broadcast_in_dim.13.b1_ref = f32[1,768]{1,0:T(1,128)} reshape(f32[768]{0:T(1024)} %param.14) | data formatting | bytes 6144 | tf_op jit(solution)/shard_map/broadcast_in_dim | solution.py:451
  3.8 1.3 %broadcast_in_dim.14.g2_ref = f32[1,768]{1,0:T(1,128)} reshape(f32[768]{0:T(1024)} %param.15) | data formatting | bytes 6144 | tf_op jit(solution)/shard_map/broadcast_in_dim | solution.py:451
  5.0 1.3 %broadcast_in_dim.15.b2_ref = f32[1,896]{1,0:T(1,128)} reshape(f32[896]{0:T(1024)} %param.18) | data formatting | bytes 7168 | tf_op jit(solution)/shard_map/broadcast_in_dim | solution.py:451
  6.3 8.9 %halo.1 = (bf16[2,16,768]{2,1,0:T(8,128)(2,1)}, bf16[2,16,768]{2,1,0:T(8,128)(2,1)}, bf16[2,16,896]{2,1,0:T(8,128)(2,1)}, bf16[2,16,896]{2,1,0:T(8,128)(2,1)}) custom-call(bf16[2,512,768]{2,1,0:T(8,128)(2,1)} %x_ref.3, bf16[2,128,896]{2,1,0:T(8,128)(2,1)} %c_ref.3), custom_call_target="tpu_custom_call" | custom-call | tf_op jit(solution)/shard_map/halo/pallas_call | solution.py:399
  15.2 32.6 %local.1 = (bf16[2,512,768]{2,1,0:T(8,128)(2,1)}, bf16[2,2,4,104,768]{4,3,2,1,0:T(8,128)(2,1)}, f32[16,896]{1,0:T(8,128)}) custom-call(s32[2]{0:T(128)} %add_convert_fusion.edge_ref, bf16[2,512,768]{2,1,0:T(8,128)(2,1)} %x_ref.3, bf16[2,16,768]{2,1,0:T(8,128)(2,1)} %get-tuple-element.18.xb_ref, bf16[2,16,768]{2,1,0:T(8,128)(2,1)} %get-tuple-element.19.xa_ref, ...), custom_call_target="tpu_custom_call" | custom-call | tf_op jit(solution)/shard_map/local/pallas_call | solution.py:418
  47.8 0.0 copy-start
  47.8 1.7 %copy-done = bf16[2,2,4,104,768]{4,3,2,1,0:T(8,128)(2,1)S(1)} copy-done((bf16[2,2,4,104,768]{4,3,2,1,0:T(8,128)(2,1)S(1)}, bf16[2,2,4,104,768]{4,3,2,1,0:T(8,128)(2,1)}, u32[]{:S(2)}) %copy-start) | copy-done | bytes 2555928
  49.5 0.0 copy-start.1
  49.5 0.8 copy-done.1
  50.4 31.8 %sums.1 = (f32[104,768]{1,0:T(8,128)S(1)}, f32[16,896]{1,0:T(8,128)S(1)}) custom-call(bf16[2,2,4,104,768]{4,3,2,1,0:T(8,128)(2,1)S(1)} %copy-done, f32[16,896]{1,0:T(8,128)S(1)} %copy-done.1), custom_call_target="tpu_custom_call" | custom-call | tf_op jit(solution)/shard_map/sums/pallas_call | solution.py:456
  82.1 0.6 slice_reduce_fusion
  82.7 0.6 slice_reduce_fusion.1
  83.4 0.6 fusion
  84.0 0.7 slice_bitcast_fusion.1
  84.6 0.7 slice_bitcast_fusion
Async XLA Ops:
  47.8 1.7 %copy-start = (bf16[2,2,4,104,768]{4,3,2,1,0:T(8,128)(2,1)S(1)}, bf16[2,2,4,104,768]{4,3,2,1,0:T(8,128)(2,1)}, u32[]{:S(2)}) copy-start(bf16[2,2,4,104,768]{4,3,2,1,0:T(8,128)(2,1)} %get-tuple-element.23.blk) | copy-start | bytes 7667716
  49.5 0.8 copy-start.1

commit v2 on v1

v2 whole, which is shorter than its diff:
```python
import functools
import math

import jax
import jax.numpy as jnp
from jax import lax
from jax.experimental import pallas as pl
from jax.experimental.pallas import tpu as pltpu
from jax.sharding import PartitionSpec as P

MESH = pl.DeviceIdType.MESH
F32 = jnp.float32
BF16 = jnp.bfloat16
epsilon = 1e-06
inv_sqrt_two = 0.7071067811865476
inv_sqrt_tau = 0.3989422804014327
HALO = 16
LANES = 128


def gelu_parts(v):
    cdf = 0.5 * (1.0 + lax.erf(v * inv_sqrt_two))
    return cdf, jnp.exp(-0.5 * v * v) * inv_sqrt_tau


def extend(planes):
    m, rows = len(planes), planes[0].shape[0]
    down = [pltpu.roll(planes[i], 1, 0) for i in (m - 2, m - 1)]
    up = [pltpu.roll(planes[i], rows - 1, 0) for i in (0, 1)]
    return down + planes + up


def step_kernel(
    scale,
    n,
    blocks,
    x_ref,
    g1_in,
    k1_ref,
    w1_hbm,
    b1_in,
    g2_in,
    k2_ref,
    w2_hbm,
    b2_in,
    c_ref,
    out_ref,
    *rest,
):
    if blocks:
        sum1_ref, sum2_ref, small_out = rest[:3]
    else:
        gt1_ref, gt2_ref, small_out = rest[:3]
    (xs, xp, fac, conv, slope, up, fac2, conv2, back2, own2, into2, cot, ss, own, inside,
     back, own1, into, dn, gt, xb_ref, xa_ref, cb_ref, ca_ref, w1_ref, w2_ref,
     g1_ref, b1_ref, g2_ref, b2_ref, small_ref, halo_send, halo_recv, load_sem) = rest[3:37]
    rest = rest[37:]
    batch, length, ch = x_ref.shape
    ch2 = c_ref.shape[2]
    span = length + 2 * HALO
    per = span // 4
    rows = batch * per
    groups = ch // LANES
    side = HALO // 4

    me = lax.axis_index("seq")
    right, left = lax.rem(me + 1, n), lax.rem(me + n - 1, n)
    others = [left, right]
    if blocks:
        z, y, core = me // 4, lax.rem(me // 2, 2), lax.rem(me, 2)
        hops = [(lax.rem(z + s, 4), lax.rem(z + s, 4) * 4 + y * 2 + core) for s in range(4)]
        mate, over = me + 1 - 2 * core, me + 2 - 4 * y
        others += [mate, over] + [hops[s][1] for s in (1, 2, 3)]
    loads = [
        pltpu.make_async_copy(w1_hbm, w1_ref, load_sem.at[0]),
        pltpu.make_async_copy(w2_hbm, w2_ref, load_sem.at[1]),
    ]
    barrier = pltpu.get_barrier_semaphore()
    for other in others:
        pl.semaphore_signal(barrier, inc=1, device_id={"seq": other}, device_id_type=MESH)
    for load in loads:
        load.start()
    for source, target in ((g1_in, g1_ref), (b1_in, b1_ref), (g2_in, g2_ref), (b2_in, b2_ref)):
        target[...] = source[...].reshape(target.shape)
    pl.semaphore_wait(barrier, len(others))

    def send(source, target, sems, k, other):
        copy = pltpu.make_async_remote_copy(
            src_ref=source,
            dst_ref=target,
            send_sem=sems[0].at[k],
            recv_sem=sems[1].at[k],
            device_id={"seq": other},
            device_id_type=MESH,
        )
        copy.start()
        return copy

    halo = []
    for ref, before, after in ((x_ref, xb_ref, xa_ref), (c_ref, cb_ref, ca_ref)):
        last = ref.shape[1] - HALO
        for source, target, other in (
            (ref.at[:, pl.ds(last, HALO)], before, right),
            (ref.at[:, pl.ds(0, HALO)], after, left),
        ):
            halo.append(send(source, target, (halo_send, halo_recv), len(halo), other))

    within = lax.broadcasted_iota(jnp.int32, (rows, LANES), 0)
    for b in range(1, batch):
        within = jnp.where(within >= per, within - per, within)
    is_own = (within >= side) & (within < per - side)
    own[...] = jnp.where(is_own, 1.0, 0.0)
    at_first, at_last = me == 0, me == n - 1
    low = jnp.where(at_first, side, 0)
    high = jnp.where(at_last, per - side, per)
    inside[...] = jnp.where((within >= low) & (within < high), 1.0, 0.0)
    def lanes(c, width=LANES):
        return pl.ds(pl.multiple_of(c * width, width), width)

    ss[...] = jnp.zeros_like(ss)
    small_ref[...] = jnp.zeros_like(small_ref)

    @pl.loop(0, groups)
    def _(c):
        for b in range(batch):
            base = b * span + HALO
            xs[c, base : base + length] = x_ref[b, :, lanes(c)].astype(F32)

    for b in range(batch):
        cot[b * per + side : (b + 1) * per - side] = c_ref[b].astype(F32) * 0.5
    for copy in halo:
        copy.wait()

    for b in range(batch):
        base = b * per
        first = cb_ref[b].astype(F32)[HALO - side :] * 0.5
        last = ca_ref[b].astype(F32)[:side] * 0.5
        cot[base : base + side] = jnp.where(at_first, 0.0, first)
        cot[base + per - side : base + per] = jnp.where(at_last, 0.0, last)


    @pl.loop(0, groups)
    def _(c):
        for b in range(batch):
            base = b * span
            xs[c, base : base + HALO] = jnp.where(at_first, 0.0, xb_ref[b, :, lanes(c)].astype(F32))
            xs[c, base + HALO + length : base + span] = jnp.where(
                at_last, 0.0, xa_ref[b, :, lanes(c)].astype(F32)
            )
        for r in range(4):
            v = xs[c, pl.ds(r, rows, stride=4), :]
            xp[r * rows : (r + 1) * rows, lanes(c)] = v
            ss[r * rows : (r + 1) * rows] += v * v

    fac[...] = jnp.broadcast_to(
        lax.rsqrt(jnp.sum(ss[...], axis=1, keepdims=True) * (1.0 / ch) + epsilon), fac.shape
    )

    def normed(values, factors, gain_ref, c, m):
        gain = gain_ref[:, lanes(c)]
        return [
            values[r * rows : (r + 1) * rows, lanes(c)] * factors[r * rows : (r + 1) * rows] * gain
            for r in range(m)
        ]

    def taps(c, m, values, factors, gain_ref, kernel_ref, target):
        ext = extend(normed(values, factors, gain_ref, c, m))
        k = [kernel_ref[j : j + 1, lanes(c)] for j in range(5)]
        for r in range(m):
            total = k[0] * ext[r]
            for j in range(1, 5):
                total = total + k[j] * ext[r + j]
            target[r * rows : (r + 1) * rows, lanes(c)] = total.astype(BF16)

    pl.loop(0, groups)(lambda c: taps(c, 4, xp, fac, g1_ref, k1_ref, conv))

    for load in loads:
        load.wait()

    wide = 256

    for t in range(2):

        @pl.loop(0, ch // wide)
        def _(n):
            part = lanes(n, wide)
            pre = jnp.dot(
                conv[2 * t * rows : 2 * (t + 1) * rows], w1_ref[:, part], preferred_element_type=F32
            )
            pre = pre + b1_ref[:, part]
            cdf, density = gelu_parts(pre)
            slope[2 * t * rows : 2 * (t + 1) * rows, part] = cdf + pre * density
            s = xp[2 * t * rows : 2 * (t + 1) * rows, part] + pre * cdf
            pooled = (s[:rows] + s[rows:]) * 0.5
            mask = inside[...]
            mask = jnp.concatenate([mask] * (wide // LANES), axis=1)
            up[t * rows : (t + 1) * rows, part] = (pooled.astype(BF16).astype(F32)) * mask

    total = jnp.zeros((2 * rows, LANES), F32)
    for c in range(groups):
        v = up[:, c * LANES : (c + 1) * LANES]
        total = total + v * v
    fac2[...] = jnp.broadcast_to(
        lax.rsqrt(jnp.sum(total, axis=1, keepdims=True) * (1.0 / ch) + epsilon), fac2.shape
    )
    pl.loop(0, groups)(lambda c: taps(c, 2, up, fac2, g2_ref, k2_ref, conv2))

    @pl.loop(0, ch2 // LANES)
    def _(n):
        part = lanes(n)
        pre = jnp.dot(conv2[...], w2_ref[:, part], preferred_element_type=F32) + b2_ref[:, part]
        cdf, density = gelu_parts(pre)
        grad = cot[:, part]
        total = jnp.zeros((1, LANES), F32)
        for t in range(2):
            at = slice(t * rows, (t + 1) * rows)
            value = (grad * (cdf[at] + pre[at] * density[at])).astype(BF16)
            back2[at, part] = value
            kept = value.astype(F32) * own[...]
            own2[at, part] = kept.astype(BF16)
            total = total + jnp.sum(kept, axis=0, keepdims=True)
        small_ref[14:15, part] = total * scale

    nt = (((1,), (1,)), ((), ()))
    tn = (((0,), (0,)), ((), ()))

    @pl.loop(0, ch // wide)
    def _(n):
        into2[:, lanes(n, wide)] = lax.dot_general(
            back2[...], w2_ref[lanes(n, wide), :], nt, preferred_element_type=F32
        ).astype(BF16)

    def weight_term(left, right, plain_ref, blk):
        for s in range(0, left.shape[1], wide):
            e = min(s + wide, left.shape[1])
            gt[s:e] = (
                lax.dot_general(left[:, s:e], right[...], tn, preferred_element_type=F32) * scale
            )
        count = left.shape[1]
        if blocks:
            size = count // 16
            for d in range(16):
                blk[d % 2, (d // 2) % 2, d // 4] = gt[d * size : (d + 1) * size].astype(BF16)
        else:
            plain_ref[...] = gt[0:count]

    if blocks:
        sums = (rest[0:9], rest[9:18])
        srecv1, ssend2, srecv2, sall, small_send, small_recv = rest[18:24]
        steps = (2, 1, 3, 0)
        flight = {}

        def stage_core(m):
            blk, recv1, sems = sums[m][0], sums[m][1], sums[m][7:9]
            flight[m] = [
                send(blk.at[1 - core, 1 - y], recv1.at[0], sems, 0, mate),
                send(blk.at[1 - core, y], recv1.at[1], sems, 1, mate),
            ]

        def stage_y(m):
            blk, recv1, kept, send2, recv2 = sums[m][:5]
            far, near = flight[m]
            far.wait()
            moving = []
            for i, step in enumerate(steps):
                zt = hops[step][0]
                send2[i] = (blk[core, 1 - y, zt].astype(F32) + recv1[0, zt].astype(F32)).astype(BF16)
                moving.append(send(send2.at[i], recv2.at[i], sums[m][7:9], 2 + i, over))
            near.wait()
            for i, step in enumerate(steps):
                zt = hops[step][0]
                kept[i] = blk[core, y, zt].astype(F32) + recv1[1, zt].astype(F32)
            flight[m] = moving

        def stage_z(m):
            kept, recv2, send3, recv3 = sums[m][2], sums[m][4], sums[m][5], sums[m][6]
            moving = []
            for i, step in enumerate(steps):
                flight[m][i].wait()
                if step:
                    send3[i] = (kept[i] + recv2[i].astype(F32)).astype(BF16)
                    moving.append(
                        send(send3.at[i], recv3.at[i], sums[m][7:9], 6 + i, hops[step][1])
                    )
                else:
                    kept[i] = kept[i] + recv2[i].astype(F32)
            flight[m] = moving

        def stage_end(m, target):
            kept, recv3 = sums[m][2], sums[m][6]
            for copy in flight[m]:
                copy.wait()
            target[...] = (kept[3] + recv3[0].astype(F32)) + (
                recv3[1].astype(F32) + recv3[2].astype(F32)
            )

    weight_term(own2, conv2, None if blocks else gt2_ref, sums[1][0] if blocks else None)
    if blocks:
        stage_core(1)

    def taps_back(c, m, values, factors, gain_ref, kernel_ref, grads, kernel_row, gain_row):
        norm = extend(normed(values, factors, gain_ref, c, m))
        g = [grads[r * rows : (r + 1) * rows, lanes(c)].astype(F32) for r in range(m)]
        ext = extend(g)
        k = [kernel_ref[j : j + 1, lanes(c)] for j in range(5)]
        gain = gain_ref[:, lanes(c)]
        mask = own[...]
        kept = [v * mask for v in g]
        gain_total = jnp.zeros((1, LANES), F32)
        for j in range(5):
            total = norm[j] * kept[0]
            for r in range(1, m):
                total = total + norm[r + j] * kept[r]
            small_ref[kernel_row + j : kernel_row + j + 1, lanes(c)] = (
                jnp.sum(total, axis=0, keepdims=True) * scale
            )
        gain_sum = None
        for r in range(m):
            at = slice(r * rows, (r + 1) * rows)
            d = k[0] * ext[r + 4]
            for j in range(1, 5):
                d = d + k[j] * ext[r + 4 - j]
            v = values[at, lanes(c)]
            dv = d * v
            term = dv * factors[at] * mask
            gain_sum = term if gain_sum is None else gain_sum + term
            ss[at] += dv * gain
            dn[at, lanes(c)] = d * gain
        small_ref[gain_row : gain_row + 1, lanes(c)] = (
            jnp.sum(gain_sum, axis=0, keepdims=True) * scale
        )

    ss[...] = jnp.zeros_like(ss)
    pl.loop(0, groups)(
        lambda c: taps_back(c, 2, up, fac2, g2_ref, k2_ref, into2, 5, 11)
    )
    f2 = fac2[...]
    inner2 = jnp.sum(ss[0 : 2 * rows], axis=1, keepdims=True) * (1.0 / ch)
    ss[0 : 2 * rows] = f2 * f2 * f2 * jnp.broadcast_to(inner2, f2.shape)

    if blocks:
        stage_y(1)

    @pl.loop(0, groups)
    def _(c):
        part = lanes(c)
        grad = cot[:, part]
        mask = inside[...] * 0.5
        total = jnp.zeros((1, LANES), F32)
        for t in range(2):
            at = slice(t * rows, (t + 1) * rows)
            d = fac2[at] * dn[at, part] - up[at, part] * ss[at] + grad
            d = d * mask
            up[at, part] = d
            for r in (2 * t, 2 * t + 1):
                to = slice(r * rows, (r + 1) * rows)
                value = (d * slope[to, part]).astype(BF16)
                back[to, part] = value
                kept = value.astype(F32) * own[...]
                own1[to, part] = kept.astype(BF16)
                total = total + jnp.sum(kept, axis=0, keepdims=True)
        small_ref[13:14, part] = total * scale

    weight_term(own1, conv, None if blocks else gt1_ref, sums[0][0] if blocks else None)
    if blocks:
        stage_core(0)

    @pl.loop(0, ch // wide)
    def _(n):
        into[:, lanes(n, wide)] = lax.dot_general(
            back[...], w1_ref[lanes(n, wide), :], nt, preferred_element_type=F32
        ).astype(BF16)

    if blocks:
        stage_z(1)
        stage_y(0)

    ss[...] = jnp.zeros_like(ss)
    pl.loop(0, groups)(lambda c: taps_back(c, 4, xp, fac, g1_ref, k1_ref, into, 0, 10))
    if blocks:
        small_sems = (small_send, small_recv)
        small_move = send(small_ref, srecv1, small_sems, 0, mate)
        stage_z(0)
    f1 = fac[...]
    inner = jnp.sum(ss[...], axis=1, keepdims=True) * (1.0 / ch)
    ss[...] = f1 * f1 * f1 * jnp.broadcast_to(inner, f1.shape)
    def finish(c):
        part = lanes(c)
        for r in range(4):
            at = slice(r * rows, (r + 1) * rows)
            half = slice((r // 2) * rows, (r // 2 + 1) * rows)
            v = up[half, part] + fac[at] * dn[at, part] - xp[at, part] * ss[at]
            xs[c, pl.ds(r, rows, stride=4), :] = v
        for b in range(batch):
            base = b * span + HALO
            out_ref[b, :, part] = xs[c, base : base + length].astype(BF16)

    middle = groups // 2
    pl.loop(0, middle)(finish)
    if blocks:
        small_move.wait()
        ssend2[...] = small_ref[...] + srecv1[...]
        small_move = send(ssend2, srecv2, small_sems, 1, over)
    pl.loop(middle, groups)(finish)
    if blocks:
        small_move.wait()
        sall[z] = ssend2[...] + srecv2[...]
        small_moves = [
            send(sall.at[z], sall.at[z], small_sems, 1 + s, hops[s][1]) for s in (1, 2, 3)
        ]
        stage_end(1, sum2_ref)
        stage_end(0, sum1_ref)
        for copy in small_moves:
            copy.wait()
        small_out[...] = (sall[0] + sall[1]) + (sall[2] + sall[3])
    else:
        small_out[...] = small_ref[...]


def sums_scratch(ch, ch2, small_shape):
    shapes = []
    for size in (ch // 16, ch2 // 16):
        shapes += [
            pltpu.VMEM((2, 2, 4, size, ch), BF16),
            pltpu.VMEM((2, 4, size, ch), BF16),
            pltpu.VMEM((4, size, ch), F32),
            pltpu.VMEM((4, size, ch), BF16),
            pltpu.VMEM((4, size, ch), BF16),
            pltpu.VMEM((3, size, ch), BF16),
            pltpu.VMEM((3, size, ch), BF16),
            pltpu.SemaphoreType.DMA((9,)),
            pltpu.SemaphoreType.DMA((9,)),
        ]
    shapes += [pltpu.VMEM(small_shape, F32)] * 3 + [pltpu.VMEM((4,) + small_shape, F32)]
    return shapes + [pltpu.SemaphoreType.DMA((5,)), pltpu.SemaphoreType.DMA((5,))]


def per_device(fast, n, x, g1, k1, w1, b1, g2, k2, w2, b2, cot):
    batch, length, ch = x.shape
    quarter, ch2 = cot.shape[1:]
    scale = 1.0 / math.sqrt(batch * length * n)
    any_spec = pl.BlockSpec(memory_space=pl.ANY)
    vmem = pl.BlockSpec(memory_space=pltpu.VMEM)

    rows = batch * (length + 2 * HALO) // 4
    small_shape = (16, ch2)
    if fast:
        grads = [jax.ShapeDtypeStruct((k // 16, ch), F32) for k in (ch, ch2)]
    else:
        grads = [jax.ShapeDtypeStruct((ch, ch), F32), jax.ShapeDtypeStruct((ch2, ch), F32)]
    outs = pl.pallas_call(
        functools.partial(step_kernel, scale, n, fast),
        out_shape=[jax.ShapeDtypeStruct(x.shape, BF16)]
        + grads
        + [jax.ShapeDtypeStruct(small_shape, F32)],
        in_specs=[vmem] * 3 + [any_spec] + [vmem] * 3 + [any_spec] + [vmem] * 2,
        out_specs=[vmem] * (2 + len(grads)),
        scratch_shapes=[
            pltpu.VMEM((ch // LANES, 4 * rows, LANES), F32),
            pltpu.VMEM((4 * rows, ch), F32),
            pltpu.VMEM((4 * rows, LANES), F32),
            pltpu.VMEM((4 * rows, ch), BF16),
            pltpu.VMEM((4 * rows, ch), F32),
            pltpu.VMEM((2 * rows, ch), F32),
            pltpu.VMEM((2 * rows, LANES), F32),
            pltpu.VMEM((2 * rows, ch), BF16),
            pltpu.VMEM((2 * rows, ch2), BF16),
            pltpu.VMEM((2 * rows, ch2), BF16),
            pltpu.VMEM((2 * rows, ch), BF16),
            pltpu.VMEM((rows, ch2), F32),
            pltpu.VMEM((4 * rows, LANES), F32),
            pltpu.VMEM((rows, LANES), F32),
            pltpu.VMEM((rows, LANES), F32),
            pltpu.VMEM((4 * rows, ch), BF16),
            pltpu.VMEM((4 * rows, ch), BF16),
            pltpu.VMEM((4 * rows, ch), BF16),
            pltpu.VMEM((4 * rows, ch), F32),
            pltpu.VMEM((max(ch, ch2), ch), F32),
            pltpu.VMEM((batch, HALO, ch), BF16),
            pltpu.VMEM((batch, HALO, ch), BF16),
            pltpu.VMEM((batch, HALO, ch2), BF16),
            pltpu.VMEM((batch, HALO, ch2), BF16),
            pltpu.VMEM(w1.shape, BF16),
            pltpu.VMEM(w2.shape, BF16),
            pltpu.VMEM((1, ch), F32),
            pltpu.VMEM((1, ch), F32),
            pltpu.VMEM((1, ch), F32),
            pltpu.VMEM((1, ch2), F32),
            pltpu.VMEM(small_shape, F32),
            pltpu.SemaphoreType.DMA((4,)),
            pltpu.SemaphoreType.DMA((4,)),
            pltpu.SemaphoreType.DMA((2,)),
        ]
        + (sums_scratch(ch, ch2, small_shape) if fast else []),
        compiler_params=pltpu.CompilerParams(
            collective_id=0, has_side_effects=True, vmem_limit_bytes=58 * 2**20
        ),
        name="step",
    )(x, g1, k1, w1, b1, g2, k2, w2, b2, cot)
    grad_x, *parts, small = outs
    if fast:
        grad_w1, grad_w2 = parts[0].T, parts[1].T
    else:
        grad_w1, grad_w2 = [
            lax.psum_scatter(part, "seq", scatter_dimension=0, tiled=True).T for part in parts
        ]
        small = lax.psum(small, "seq")
    return (
        grad_x,
        grad_w1,
        grad_w2,
        small[13, :ch],
        small[14],
        small[0:5, :ch],
        small[5:10, :ch],
        small[10, :ch],
        small[11, :ch],
    )


def solution(mesh):
    n = mesh.shape["seq"]
    return jax.shard_map(
        functools.partial(per_device, n == 16, n),
        mesh=mesh,
        in_specs=(P("groups", "seq", None),) + (P(),) * 8 + (P("groups", "seq", None),),
        out_specs=(
            P("groups", "seq", None),
            P("groups", "seq"),
            P("groups", "seq"),
            P("groups"),
            P("groups"),
            P("groups", None),
            P("groups", None),
            P("groups"),
            P("groups"),
        ),
        check_vma=False,
    )
```

time: 85.7 us -> 65.1 us (0.76)
  Pallas kernels: 73.3 us -> 55.7 us
  local copies, waits for them, and re-layouts: 10.8 us -> 8.32 us
    pallas_call x3 -> x1, Pallas kernels: 73.3 us -> 55.7 us  [per_device(): pl.pallas_call(functools.partial(step_kernel, scale, n, fast), out_shape=...]
    broadcast_in_dim x4 -> x0, local copies, waits for them, and re-layouts: 5.07 us -> none  [the longest x1 1.27 us: per_device(): b2[None]]
    unnamed x4 -> x7, local copies, waits for them, and re-layouts: 2.54 us -> 4.04 us
    transpose x2 -> x0, local copies, waits for them, and re-layouts: 1.35 us -> none  [per_device(): grad_w1, grad_w2 = (total[:ch // 16].T, total[ch // 16:].T)]
    slice x1, local copies, waits for them, and re-layouts: 0.62 us -> 1.49 us  [per_device(): small[11, :ch]]
where the time goes in v2:
time: 65.1 us; the launch traced here: 64.7 us
  Pallas kernels  55.7 us (86%)
  local copies, waits for them, and re-layouts  8.32 us (13%)
  between operations  0.66 us (1%)
    pallas_call x1, Pallas kernels, per_device(): pl.pallas_call(functools.partial(step_kernel, scale, n, fast), out_shape=...  55.7 us
    unnamed x7, local copies, waits for them, and re-layouts  4.04 us
    slice x1, local copies, waits for them, and re-layouts, per_device(): small[11, :ch]  1.49 us
    slice x1, local copies, waits for them, and re-layouts, per_device(): small[5:10, :ch]  1.43 us
    slice x1, local copies, waits for them, and re-layouts, per_device(): small[14]  1.35 us

profile of v2, /device:TPU:0, one launch (start us, length us, event | category | flops | bytes accessed | tf_op | source)
XLA Modules:
  0.0 64.7 jit_solution(7035785182123985353)
XLA Ops:
  0.6 55.7 %step.1 = (bf16[2,512,768]{2,1,0:T(8,128)(2,1)}, f32[48,768]{1,0:T(8,128)}, f32[56,768]{1,0:T(8,128)}, f32[16,896]{1,0:T(8,128)}) custom-call(bf16[2,512,768]{2,1,0:T(8,128)(2,1)} %x_ref.1, f32[768]{0:T(1024)} %g1_in.1, f32[5,768]{1,0:T(8,128)} %k1_ref.1, bf16[768,768]{1,0:T(8,128)(2,1)} %w1_hbm.1, f32[768]{0:T(1024)} %b1_in.1, f32[768]{0:T(1024)} %g2_in.1, ...), custom_call_target="tpu_custom_call" | custom-call | tf_op jit(solution)/shard_map/step/pallas_call | solution.py:451
  56.4 1.4 %slice_reduce_fusion = f32[896]{0:T(1024)} fusion(f32[16,896]{1,0:T(8,128)} %get-tuple-element.16), kind=kLoop, calls=%fused_computation | loop fusion | bytes 7168 | tf_op jit(solution)/shard_map/slice | solution.py:513
  57.7 1.5 %slice_reduce_fusion.1 = (f32[768]{0:T(1024)}, f32[768]{0:T(1024)}, f32[768]{0:T(1024)}) fusion(f32[16,896]{1,0:T(8,128)} %get-tuple-element.16), kind=kLoop, calls=%fused_computation.1 | loop fusion | bytes 18432 | tf_op jit(solution)/shard_map/slice | solution.py:517
  59.2 1.4 %fusion = (f32[5,768]{1,0:T(8,128)}, f32[5,768]{1,0:T(8,128)}) fusion(f32[16,896]{1,0:T(8,128)} %get-tuple-element.16), kind=kLoop, calls=%fused_computation.4 | loop fusion | bytes 61440 | tf_op jit(solution)/shard_map/slice | solution.py:515
  60.6 0.0 copy-start.1
  60.6 0.0 copy-start
  60.7 2.7 %copy.22 = bf16[2,512,768]{2,1,0:T(8,128)(2,1)} copy(bf16[2,512,768]{2,1,0:T(8,128)(2,1)} %get-tuple-element.31) | data formatting | bytes 3145728
  63.4 0.0 copy-done.1
  63.4 0.7 %copy.23 = f32[768,48]{0,1:T(8,128)} copy(f32[768,48]{0,1:T(8,128)S(1)} %bitcast.3) | data formatting | bytes 294912
  64.0 0.0 copy-done
  64.0 0.7 %copy.24 = f32[768,56]{0,1:T(8,128)} copy(f32[768,56]{0,1:T(8,128)S(1)} %bitcast.2) | data formatting | bytes 344064
Async XLA Ops:
  60.6 2.7 %copy-start.1 = (f32[48,768]{1,0:T(8,128)S(1)}, f32[48,768]{1,0:T(8,128)}, u32[]{:S(2)}) copy-start(f32[48,768]{1,0:T(8,128)} %get-tuple-element.14) | copy-start | bytes 442372
  60.6 3.4 %copy-start = (f32[56,768]{1,0:T(8,128)S(1)}, f32[56,768]{1,0:T(8,128)}, u32[]{:S(2)}) copy-start(f32[56,768]{1,0:T(8,128)} %get-tuple-element.15) | copy-start | bytes 516100

commit v3 on v2

--- a/solution.py
+++ b/solution.py
@@ -84,8 +84,8 @@
         target[...] = source[...].reshape(target.shape)
     pl.semaphore_wait(barrier, len(others))
 
-    def send(source, target, sems, k, other):
-        copy = pltpu.make_async_remote_copy(
+    def remote(source, target, sems, k, other):
+        return pltpu.make_async_remote_copy(
             src_ref=source,
             dst_ref=target,
             send_sem=sems[0].at[k],
@@ -93,6 +93,9 @@
             device_id={"seq": other},
             device_id_type=MESH,
         )
+
+    def send(*args):
+        copy = remote(*args)
         copy.start()
         return copy
 
@@ -261,35 +264,32 @@
             blk, recv1, kept, send2, recv2 = sums[m][:5]
             far, near = flight[m]
             far.wait()
-            moving = []
             for i, step in enumerate(steps):
                 zt = hops[step][0]
                 send2[i] = (blk[core, 1 - y, zt].astype(F32) + recv1[0, zt].astype(F32)).astype(BF16)
-                moving.append(send(send2.at[i], recv2.at[i], sums[m][7:9], 2 + i, over))
+                send(send2.at[i], recv2.at[i], sums[m][7:9], 2 + i, over)
             near.wait()
             for i, step in enumerate(steps):
                 zt = hops[step][0]
                 kept[i] = blk[core, y, zt].astype(F32) + recv1[1, zt].astype(F32)
-            flight[m] = moving
-
-        def stage_z(m):
-            kept, recv2, send3, recv3 = sums[m][2], sums[m][4], sums[m][5], sums[m][6]
-            moving = []
-            for i, step in enumerate(steps):
-                flight[m][i].wait()
-                if step:
-                    send3[i] = (kept[i] + recv2[i].astype(F32)).astype(BF16)
-                    moving.append(
-                        send(send3.at[i], recv3.at[i], sums[m][7:9], 6 + i, hops[step][1])
-                    )
-                else:
-                    kept[i] = kept[i] + recv2[i].astype(F32)
-            flight[m] = moving
+
+        def z_copy(m, i):
+            send3, recv3, sems = sums[m][5], sums[m][6], sums[m][7:9]
+            return remote(send3.at[i], recv3.at[i], sems, 6 + i, hops[steps[i]][1])
+
+        def stage_z(m, i):
+            kept, recv2, send3 = sums[m][2], sums[m][4], sums[m][5]
+            remote(sums[m][3].at[i], recv2.at[i], sums[m][7:9], 2 + i, over).wait()
+            if steps[i]:
+                send3[i] = (kept[i] + recv2[i].astype(F32)).astype(BF16)
+                z_copy(m, i).start()
+            else:
+                kept[i] = kept[i] + recv2[i].astype(F32)
 
         def stage_end(m, target):
             kept, recv3 = sums[m][2], sums[m][6]
-            for copy in flight[m]:
-                copy.wait()
+            for i in range(3):
+                z_copy(m, i).wait()
             target[...] = (kept[3] + recv3[0].astype(F32)) + (
                 recv3[1].astype(F32) + recv3[2].astype(F32)
             )
@@ -372,15 +372,22 @@
         ).astype(BF16)
 
     if blocks:
-        stage_z(1)
+        for i in range(4):
+            stage_z(1, i)
         stage_y(0)
 
     ss[...] = jnp.zeros_like(ss)
-    pl.loop(0, groups)(lambda c: taps_back(c, 4, xp, fac, g1_ref, k1_ref, into, 0, 10))
+
+    @pl.loop(0, groups)
+    def _(c):
+        taps_back(c, 4, xp, fac, g1_ref, k1_ref, into, 0, 10)
+        if blocks:
+            for i in range(4):
+                pl.when(c == groups - 4 + i)(functools.partial(stage_z, 0, i))
+
     if blocks:
         small_sems = (small_send, small_recv)
         small_move = send(small_ref, srecv1, small_sems, 0, mate)
-        stage_z(0)
     f1 = fac[...]
     inner = jnp.sum(ss[...], axis=1, keepdims=True) * (1.0 / ch)
     ss[...] = f1 * f1 * f1 * jnp.broadcast_to(inner, f1.shape)
@@ -390,10 +397,7 @@
             at = slice(r * rows, (r + 1) * rows)
             half = slice((r // 2) * rows, (r // 2 + 1) * rows)
             v = up[half, part] + fac[at] * dn[at, part] - xp[at, part] * ss[at]
-            xs[c, pl.ds(r, rows, stride=4), :] = v
-        for b in range(batch):
-            base = b * span + HALO
-            out_ref[b, :, part] = xs[c, base : base + length].astype(BF16)
+            out_ref[at, part] = v.astype(BF16)
 
     middle = groups // 2
     pl.loop(0, middle)(finish)
@@ -415,6 +419,39 @@
         small_out[...] = (sall[0] + sall[1]) + (sall[2] + sall[3])
     else:
         small_out[...] = small_ref[...]
+
+
+def tail_kernel(fast, p_ref, small_ref, *refs):
+    if fast:
+        s1_ref, s2_ref, x_out, w1_out, w2_out = refs[:5]
+        refs = refs[5:]
+    else:
+        x_out, refs = refs[0], refs[1:]
+    b1_out, b2_out, k1_out, k2_out, g1_out, g2_out, mix = refs
+    batch, length, width = x_out.shape
+    rows = p_ref.shape[0] // 4
+    span = 4 * rows // batch
+    ch = b1_out.shape[0]
+
+    @pl.when(pl.program_id(0) == 0)
+    def _():
+        if fast:
+            w1_out[...] = s1_ref[...]
+            w2_out[...] = s2_ref[...]
+        b1_out[...] = small_ref[13, :ch]
+        b2_out[...] = small_ref[14, :]
+        k1_out[...] = small_ref[0:5, :ch]
+        k2_out[...] = small_ref[5:10, :ch]
+        g1_out[...] = small_ref[10, :ch]
+        g2_out[...] = small_ref[11, :ch]
+
+    for k in range(width // LANES):
+        part = slice(k * LANES, (k + 1) * LANES)
+        for r in range(4):
+            mix[k, pl.ds(r, rows, stride=4), :] = p_ref[r * rows : (r + 1) * rows, part].astype(F32)
+        for b in range(batch):
+            base = b * span + HALO
+            x_out[b, :, part] = mix[k, base : base + length].astype(BF16)
 
 
 def sums_scratch(ch, ch2, small_shape):
@@ -450,7 +487,7 @@
         grads = [jax.ShapeDtypeStruct((ch, ch), F32), jax.ShapeDtypeStruct((ch2, ch), F32)]
     outs = pl.pallas_call(
         functools.partial(step_kernel, scale, n, fast),
-        out_shape=[jax.ShapeDtypeStruct(x.shape, BF16)]
+        out_shape=[jax.ShapeDtypeStruct((4 * rows, ch), BF16)]
         + grads
         + [jax.ShapeDtypeStruct(small_shape, F32)],
         in_specs=[vmem] * 3 + [any_spec] + [vmem] * 3 + [any_spec] + [vmem] * 2,
@@ -497,25 +534,35 @@
         ),
         name="step",
     )(x, g1, k1, w1, b1, g2, k2, w2, b2, cot)
-    grad_x, *parts, small = outs
-    if fast:
-        grad_w1, grad_w2 = parts[0].T, parts[1].T
-    else:
-        grad_w1, grad_w2 = [
+    planes, *parts, small = outs
+    if not fast:
+        grad_w = [
             lax.psum_scatter(part, "seq", scatter_dimension=0, tiled=True).T for part in parts
         ]
         small = lax.psum(small, "seq")
-    return (
-        grad_x,
-        grad_w1,
-        grad_w2,
-        small[13, :ch],
-        small[14],
-        small[0:5, :ch],
-        small[5:10, :ch],
-        small[10, :ch],
-        small[11, :ch],
-    )
+        parts = []
+
+    def whole(shape):
+        return pl.BlockSpec(shape, lambda i: (0,) * len(shape))
+
+    width = 2 * LANES
+    results = [part.shape for part in parts]
+    results += [(ch,), (ch2,), (5, ch), (5, ch), (ch,), (ch,)]
+    grad_x, *rest = pl.pallas_call(
+        functools.partial(tail_kernel, fast),
+        grid=(ch // width,),
+        out_shape=[jax.ShapeDtypeStruct(x.shape, BF16)]
+        + [jax.ShapeDtypeStruct(shape, F32) for shape in results],
+        in_specs=[pl.BlockSpec((4 * rows, width), lambda i: (0, i)), whole(small_shape)]
+        + [whole(part.shape) for part in parts],
+        out_specs=[pl.BlockSpec((batch, length, width), lambda i: (0, 0, i))]
+        + [whole(shape) for shape in results],
+        scratch_shapes=[pltpu.VMEM((width // LANES, 4 * rows, LANES), F32)],
+        name="tail",
+    )(planes, small, *parts)
+    if fast:
+        grad_w, rest = [part.T for part in rest[:2]], rest[2:]
+    return (grad_x, *grad_w, *rest)
 
 
 def solution(mesh):

time: 65.1 us -> 60.7 us (0.932)
  local copies, waits for them, and re-layouts: 8.32 us -> 0 us
  Pallas kernels: 55.7 us -> 59.8 us
    slice x3 -> x0, local copies, waits for them, and re-layouts: 4.28 us -> none  [the longest x1 1.49 us: per_device(): small[11, :ch]]
    unnamed x7 -> x0, local copies, waits for them, and re-layouts: 4.04 us -> none
    pallas_call x0 -> x1, Pallas kernels: none -> 3.87 us  [per_device(): pl.pallas_call(functools.partial(tail_kernel, fast), grid=(ch // width,),...]
where the time goes in v3:
time: 60.7 us; the launch traced here: 60.5 us
  Pallas kernels  59.8 us (99%)
  between operations  0.65 us (1%)
    pallas_call x1, Pallas kernels, per_device(): pl.pallas_call(functools.partial(step_kernel, scale, n, fast), out_shape=...  56 us
    pallas_call x1, Pallas kernels, per_device(): pl.pallas_call(functools.partial(tail_kernel, fast), grid=(ch // width,),...  3.87 us

profile of v3, /device:TPU:0, one launch (start us, length us, event | category | flops | bytes accessed | tf_op | source)
XLA Modules:
  0.0 60.5 jit_solution(17728314066100747640)
XLA Ops:
  0.6 56.0 %step.1 = (bf16[1088,768]{1,0:T(8,128)(2,1)}, f32[48,768]{1,0:T(8,128)}, f32[56,768]{1,0:T(8,128)}, f32[16,896]{1,0:T(8,128)}) custom-call(bf16[2,512,768]{2,1,0:T(8,128)(2,1)} %x_ref.1, f32[768]{0:T(1024)} %g1_in.1, f32[5,768]{1,0:T(8,128)} %k1_ref.1, bf16[768,768]{1,0:T(8,128)(2,1)} %w1_hbm.1, f32[768]{0:T(1024)} %b1_in.1, f32[768]{0:T(1024)} %g2_in.1, ...), custom_call_target="tpu_custom_call" | custom-call | tf_op jit(solution)/shard_map/step/pallas_call | solution.py:488
  56.6 3.9 %tail.1 = (bf16[2,512,768]{2,1,0:T(8,128)(2,1)}, f32[48,768]{1,0:T(8,128)}, f32[56,768]{1,0:T(8,128)}, f32[768]{0:T(1024)}, f32[896]{0:T(1024)}, /*index=5*/f32[...) custom-call(bf16[1088,768]{1,0:T(8,128)(2,1)} %get-tuple-element.22.p_ref, ...), custom_call_target="tpu_custom_call" | custom-call | tf_op jit(solution)/shard_map/tail/pallas_call | solution.py:551

commit v4 on v3

--- a/solution.py
+++ b/solution.py
@@ -227,12 +227,6 @@
     nt = (((1,), (1,)), ((), ()))
     tn = (((0,), (0,)), ((), ()))
 
-    @pl.loop(0, ch // wide)
-    def _(n):
-        into2[:, lanes(n, wide)] = lax.dot_general(
-            back2[...], w2_ref[lanes(n, wide), :], nt, preferred_element_type=F32
-        ).astype(BF16)
-
     def weight_term(left, right, plain_ref, blk):
         for s in range(0, left.shape[1], wide):
             e = min(s + wide, left.shape[1])
@@ -297,6 +291,15 @@
     weight_term(own2, conv2, None if blocks else gt2_ref, sums[1][0] if blocks else None)
     if blocks:
         stage_core(1)
+
+    @pl.loop(0, ch // wide)
+    def _(n):
+        into2[:, lanes(n, wide)] = lax.dot_general(
+            back2[...], w2_ref[lanes(n, wide), :], nt, preferred_element_type=F32
+        ).astype(BF16)
+
+    if blocks:
+        stage_y(1)
 
     def taps_back(c, m, values, factors, gain_ref, kernel_ref, grads, kernel_row, gain_row):
         norm = extend(normed(values, factors, gain_ref, c, m))
@@ -338,9 +341,6 @@
     inner2 = jnp.sum(ss[0 : 2 * rows], axis=1, keepdims=True) * (1.0 / ch)
     ss[0 : 2 * rows] = f2 * f2 * f2 * jnp.broadcast_to(inner2, f2.shape)
 
-    if blocks:
-        stage_y(1)
-
     @pl.loop(0, groups)
     def _(c):
         part = lanes(c)
@@ -361,9 +361,13 @@
                 total = total + jnp.sum(kept, axis=0, keepdims=True)
         small_ref[13:14, part] = total * scale
 
+    if blocks:
+        stage_z(1, 0)
+
     weight_term(own1, conv, None if blocks else gt1_ref, sums[0][0] if blocks else None)
     if blocks:
         stage_core(0)
+        stage_z(1, 1)
 
     @pl.loop(0, ch // wide)
     def _(n):
@@ -372,22 +376,16 @@
         ).astype(BF16)
 
     if blocks:
-        for i in range(4):
-            stage_z(1, i)
         stage_y(0)
+        stage_z(1, 2)
 
     ss[...] = jnp.zeros_like(ss)
-
-    @pl.loop(0, groups)
-    def _(c):
-        taps_back(c, 4, xp, fac, g1_ref, k1_ref, into, 0, 10)
-        if blocks:
-            for i in range(4):
-                pl.when(c == groups - 4 + i)(functools.partial(stage_z, 0, i))
-
+    pl.loop(0, groups)(lambda c: taps_back(c, 4, xp, fac, g1_ref, k1_ref, into, 0, 10))
     if blocks:
         small_sems = (small_send, small_recv)
         small_move = send(small_ref, srecv1, small_sems, 0, mate)
+        stage_z(1, 3)
+        stage_z(0, 0)
     f1 = fac[...]
     inner = jnp.sum(ss[...], axis=1, keepdims=True) * (1.0 / ch)
     ss[...] = f1 * f1 * f1 * jnp.broadcast_to(inner, f1.shape)
@@ -405,13 +403,16 @@
         small_move.wait()
         ssend2[...] = small_ref[...] + srecv1[...]
         small_move = send(ssend2, srecv2, small_sems, 1, over)
+        stage_z(0, 1)
     pl.loop(middle, groups)(finish)
     if blocks:
+        stage_z(0, 2)
         small_move.wait()
         sall[z] = ssend2[...] + srecv2[...]
         small_moves = [
             send(sall.at[z], sall.at[z], small_sems, 1 + s, hops[s][1]) for s in (1, 2, 3)
         ]
+        stage_z(0, 3)
         stage_end(1, sum2_ref)
         stage_end(0, sum1_ref)
         for copy in small_moves:

time: 60.7 us -> 57 us (0.939)
  Pallas kernels: 59.8 us -> 56.1 us
    pallas_call x1, Pallas kernels: 56 us -> 52.3 us  [per_device(): pl.pallas_call(functools.partial(step_kernel, scale, n, fast), out_shape=...]
where the time goes in v4:
time: 57 us; the launch traced here: 56.8 us
  Pallas kernels  56.1 us (98%)
  between operations  0.65 us (1%)
    pallas_call x1, Pallas kernels, per_device(): pl.pallas_call(functools.partial(step_kernel, scale, n, fast), out_shape=...  52.3 us
    pallas_call x1, Pallas kernels, per_device(): pl.pallas_call(functools.partial(tail_kernel, fast), grid=(ch // width,),...  3.87 us

profile of v4, /device:TPU:0, one launch (start us, length us, event | category | flops | bytes accessed | tf_op | source)
XLA Modules:
  0.0 56.8 jit_solution(1455883357892273161)
XLA Ops:
  0.6 52.3 %step.1 = (bf16[1088,768]{1,0:T(8,128)(2,1)}, f32[48,768]{1,0:T(8,128)}, f32[56,768]{1,0:T(8,128)}, f32[16,896]{1,0:T(8,128)}) custom-call(bf16[2,512,768]{2,1,0:T(8,128)(2,1)} %x_ref.1, f32[768]{0:T(1024)} %g1_in.1, f32[5,768]{1,0:T(8,128)} %k1_ref.1, bf16[768,768]{1,0:T(8,128)(2,1)} %w1_hbm.1, f32[768]{0:T(1024)} %b1_in.1, f32[768]{0:T(1024)} %g2_in.1, ...), custom_call_target="tpu_custom_call" | custom-call | tf_op jit(solution)/shard_map/step/pallas_call | solution.py:489
  52.9 3.9 %tail.1 = (bf16[2,512,768]{2,1,0:T(8,128)(2,1)}, f32[48,768]{1,0:T(8,128)}, f32[56,768]{1,0:T(8,128)}, f32[768]{0:T(1024)}, f32[896]{0:T(1024)}, /*index=5*/f32[...) custom-call(bf16[1088,768]{1,0:T(8,128)(2,1)} %get-tuple-element.22.p_ref, ...), custom_call_target="tpu_custom_call" | custom-call | tf_op jit(solution)/shard_map/tail/pallas_call | solution.py:552
